TPU v7x, 128 devices: a whole 4x4x4 slice. The times are simulated.
128 devices in a mesh: det: 8 (over z, core), scan: 16 (over x, y).
Axes of the slice: x: 4, y: 4, z: 4, core: 2. Of those that a mesh axis runs over, the one named last changes fastest.
Arguments:
- intensity: bfloat16 [576, 512, 512], P('det', 'scan'), may hold values from -6 to 6
- aberrations: float32 [3], replicated, may hold values from 0.5 to 1.5
- lune_blocks: int32 [8, 16, 16], replicated, may hold values from 0 to 71, as said below
- lune_weight: int32 [8, 16, 16], replicated, may hold values from -1 to 1, as said below
Outputs:
- image: float32 [2, 512, 512], P(None, ('det', 'scan'))
Inputs may be any that keep to these rules, and one draw needn't show every extreme that they name: `lune_blocks`: each tile's list holds 16 different detector blocks. Counting a tile's blocks by detector shard (block b lies in shard b // 9), exactly one shard holds 4 of them; of the other seven shards, five hold 2 and two hold 1. `lune_weight`: every entry is -1 or +1, never 0.
All inputs are finite; a program needn't handle non-finite values.
Results may differ from a plain program's by a relative error of at most 0.0052.
Values may be sent and summed in bfloat16 or wider, within the bound.
No kernel may reach another device: no remote copies, remote signals or barrier semaphores. Data moves between devices by JAX's collectives and lax.ppermute only.
A program may use at most 256 MiB of HBM per device.

v0:
```python
import math

import jax
import jax.numpy as jnp
from jax import lax
from jax.sharding import PartitionSpec as P

DSIDE = 24
BLK = 8


freq_span = 4.0
detector_extent = 2.4
quartic_factor = 0.05


def dft_tables(length):
    counter = jnp.arange(length, dtype=jnp.int32)
    product = counter[:, None] * counter[None, :] % length
    angles = product.astype(jnp.float32) * (2.0 * math.pi / length)
    return (jnp.cos(angles), jnp.sin(angles))


def frequency(counter, length):
    shifted = (counter + length // 2) % length - length // 2
    return shifted.astype(jnp.float32) * (freq_span / length)


def detector_position(pixels):
    centre = (DSIDE - 1) / 2.0
    pitch_size = detector_extent / DSIDE
    pos_x = ((pixels % DSIDE).astype(jnp.float32) - centre) * pitch_size
    pos_y = ((pixels // DSIDE).astype(jnp.float32) - centre) * pitch_size
    return (pos_x, pos_y)


def aberration_phase(along_x, along_y, aberrations):
    radius = along_x * along_x + along_y * along_y
    return math.pi * (
        aberrations[0] * radius
        + quartic_factor * aberrations[1] * radius * radius
        + aberrations[2] * (along_x * along_x - along_y * along_y)
    )


def lune_terms(spec_re, spec_im, weight_sign, pos_x, pos_y, freq_x, freq_y, aberrations):
    phase = aberration_phase(pos_x, pos_y, aberrations) - aberration_phase(
        pos_x - weight_sign * freq_x, pos_y - weight_sign * freq_y, aberrations
    )
    cos_phase = jnp.cos(phase)
    sin_phase = jnp.sin(phase)
    real_part = weight_sign * spec_re * cos_phase - spec_im * sin_phase
    imag_part = weight_sign * spec_im * cos_phase + spec_re * sin_phase
    return (real_part, imag_part)


def shards(intensity, aberrations, lune_blocks, lune_weight):
    maximum_level = lax.Precision.HIGHEST
    pix_dev, row_dev, length = intensity.shape
    det_count = lax.axis_size("det")
    scan_count = lax.axis_size("scan")
    det_index = lax.axis_index("det")
    scan_index = lax.axis_index("scan")
    tile_rows = length // det_count
    tile_cols = length // scan_count
    blocks_dev = pix_dev // BLK
    list_length = lune_blocks.shape[2]
    cosine_table, sine_table = dft_tables(length)
    cos_low = cosine_table.astype(jnp.bfloat16)
    sin_low = sine_table.astype(jnp.bfloat16)
    table_row_count = jnp.stack([cos_low, -sin_low])
    table_cols = jnp.stack([jnp.stack([cos_low, sin_low]), jnp.stack([-sin_low, cos_low])])
    row_fourier_spectrum = jnp.einsum(
        "tlf,inf->tlin", intensity, table_row_count, preferred_element_type=jnp.float32
    ).astype(jnp.bfloat16)
    own_blocks = lune_blocks[det_index, scan_index]
    own_weight = lune_weight[det_index, scan_index]
    full_spectrum = jnp.einsum(
        "oiqr,nric->nocq",
        table_cols,
        lax.all_to_all(row_fourier_spectrum, "scan", split_axis=3, concat_axis=1, tiled=True),
        preferred_element_type=jnp.float32,
    )
    spectrum = (full_spectrum * (1.0 / length)).astype(jnp.bfloat16)
    spectrum = spectrum.reshape(blocks_dev, BLK, 2, tile_cols, det_count, tile_rows)
    arrived = lax.all_to_all(spectrum, "det", split_axis=4, concat_axis=0, tiled=True)
    selected = jnp.take(arrived[:, :, :, :, 0], own_blocks, axis=0)
    pixels = own_blocks[:, None] * BLK + jnp.arange(BLK, dtype=jnp.int32)[None, :]
    pos_x, pos_y = detector_position(pixels)
    freq_y = frequency(det_index * tile_rows + jnp.arange(tile_rows, dtype=jnp.int32), length)
    freq_x = frequency(scan_index * tile_cols + jnp.arange(tile_cols, dtype=jnp.int32), length)
    weight_sign = own_weight.astype(jnp.float32)[:, None, None, None]
    spectrum_entries = selected.astype(jnp.float32)
    real_part, imag_part = lune_terms(
        spectrum_entries[:, :, 0],
        spectrum_entries[:, :, 1],
        weight_sign,
        pos_x[:, :, None, None],
        pos_y[:, :, None, None],
        freq_x[None, None, :, None],
        freq_y[None, None, None, :],
        aberrations,
    )
    spectrum_tile = jnp.stack(
        [jnp.sum(real_part, axis=(0, 1)), jnp.sum(imag_part, axis=(0, 1))]
    ) * (1.0 / math.sqrt(list_length * BLK))
    out_rows = jnp.arange(lax.axis_size("det") * tile_rows, dtype=jnp.int32)
    tile_freq = det_index * tile_rows + jnp.arange(tile_rows, dtype=jnp.int32)
    angles = (out_rows[:, None] * tile_freq[None, :] % length).astype(jnp.float32) * (
        2.0 * math.pi / length
    )
    cos_part = jnp.cos(angles)
    sine_component = jnp.sin(angles)
    contract_dims = (((1,), (1,)), ((), ()))
    real_tile = spectrum_tile[0]
    imag_tile = spectrum_tile[1]
    back_re = lax.dot_general(
        cos_part, real_tile, contract_dims, precision=maximum_level
    ) - lax.dot_general(sine_component, imag_tile, contract_dims, precision=maximum_level)
    back_im = lax.dot_general(
        sine_component, real_tile, contract_dims, precision=maximum_level
    ) + lax.dot_general(cos_part, imag_tile, contract_dims, precision=maximum_level)
    back_rows = lax.psum_scatter(
        jnp.stack([back_re, back_im], axis=1), "det", scatter_dimension=0, tiled=True
    )
    image_rows = lax.all_to_all(back_rows, "scan", split_axis=0, concat_axis=2, tiled=True)
    image_re = (
        jnp.dot(image_rows[:, 0], cosine_table, precision=maximum_level)
        - jnp.dot(image_rows[:, 1], sine_table, precision=maximum_level)
    ) * (1.0 / length)
    image_im = (
        jnp.dot(image_rows[:, 0], sine_table, precision=maximum_level)
        + jnp.dot(image_rows[:, 1], cosine_table, precision=maximum_level)
    ) * (1.0 / length)
    return jnp.stack([image_re, image_im])


def solution(mesh):
    return jax.shard_map(
        shards,
        mesh=mesh,
        in_specs=(P("det", "scan", None), P(), P(), P()),
        out_specs=P(None, ("det", "scan"), None),
        check_vma=False,
    )
```

profile of v0, /device:TPU:1, one launch (start us, length us, event | category | flops | bytes accessed | tf_op | source)
XLA Modules:
  0.0 427.7 jit_solution(8205225915390923256)
XLA Ops:
  6.5 4.3 %sine_convert_fusion = (bf16[1,512,512]{2,1,0:T(8,128)(2,1)S(1)}, bf16[1,512,512]{2,1,0:T(8,128)(2,1)S(1)}) fusion(), kind=kLoop, calls=%fused_computation.53 | loop fusion | flops 4194304 | bytes 1048576 | tf_op jit(solution)/shard_map/convert_element_type | solution.py:70
  10.8 4.0 fusion.48
  14.9 7.2 %convert_bitcast_fusion = bf16[72,32,2,512]{3,0,1,2:T(8,128)(2,1)} fusion(bf16[72,32,512]{2,1,0:T(8,128)(2,1)} %param.4, bf16[1,512,512]{2,1,0:T(8,128)(2,1)S(1)} %get-tuple-element.20, bf16[1,512,512]{2,1,0:T(8,128)(2,1)S(1)} %fusion.48), kind=kOutput, calls=%fused_computation.4 | convolution fusion | flops 2420375552 | bytes 8126464 | tf_op jit(solution)/shard_map/tlf,inf->tlin/dot_general | solution.py:73
  22.0 13.8 %copy.26 = bf16[72,32,2,512]{0,1,2,3:T(8,128)(2,1)} copy(bf16[72,32,2,512]{3,0,1,2:T(8,128)(2,1)} %convert_bitcast_fusion) | data formatting | bytes 9437184 | tf_op jit(solution)/shard_map/convert_element_type | solution.py:75
  35.8 7.6 %all-to-all-start = ((bf16[72,32,2,512]{0,1,2,3:T(8,128)(2,1)}), bf16[72,32,2,512]{0,1,2,3:T(8,128)(2,1)}, u32[]{:S(2)}, u32[]{:S(2)}) async-start(bf16[72,32,2,512]{0,1,2,3:T(8,128)(2,1)} %copy.26), calls=%async_computation | async-start | bytes 16777216 | tf_op jit(solution)/shard_map/all_to_all | solution.py:81
  43.5 1.1 fusion.20
  44.6 144.9 %all-to-all-done = bf16[72,32,2,512]{0,1,2,3:T(8,128)(2,1)} async-done(((bf16[72,32,2,512]{0,1,2,3:T(8,128)(2,1)}), bf16[72,32,2,512]{0,1,2,3:T(8,128)(2,1)}, u32[]{:S(2)}, u32[]{:S(2)}) %all-to-all-start) | async-done | bytes 4718624 | tf_op jit(solution)/shard_map/all_to_all | solution.py:81
  189.5 13.6 %copy.28 = bf16[72,16,32,2,32]{0,4,3,2,1:T(8,128)(2,1)} copy(bf16[72,16,32,2,32]{0,2,3,4,1:T(8,128)(2,1)} %bitcast.8) | data formatting | bytes 9437184 | tf_op jit(solution)/shard_map/all_to_all | solution.py:81
  203.2 14.6 %copy.39 = bf16[72,512,2,32,1]{1,3,2,4,0:T(8,128)(2,1)} copy(bf16[72,512,2,32,1]{0,3,2,1,4:T(8,128)(2,1)} %bitcast.107) | data formatting | bytes 9437184 | tf_op jit(solution)/shard_map/all_to_all | solution.py:81
  217.7 9.1 %fusion.1 = bf16[72,2,32,512]{3,2,1,0:T(8,128)(2,1)} fusion(bf16[72,512,2,32,1]{1,3,2,4,0:T(8,128)(2,1)} %copy.39, bf16[1,2,512,512]{3,2,1,0:T(8,128)(2,1)S(1)} %copy-done, bf16[1,2,512,512]{3,2,1,0:T(8,128)(2,1)S(1)} %get-tuple-element.9), kind=kOutput, calls=%fused_computation.3 | convolution fusion | flops 4840751104 | bytes 11534336 | tf_op jit(solution)/shard_map/oiqr,nric->nocq/dot_general | solution.py:78
  226.9 12.5 %reshape.342 = bf16[9,8,2,32,8,64]{5,4,3,2,1,0:T(8,128)(2,1)} reshape(bf16[72,2,32,512]{3,2,1,0:T(8,128)(2,1)} %fusion.1) | data formatting | bytes 9437184 | tf_op jit(solution)/shard_map/reshape | solution.py:85
  239.4 9.9 %copy.72 = bf16[9,8,2,32,8,64]{5,3,2,1,0,4:T(8,128)(2,1)} copy(bf16[9,8,2,32,8,64]{5,4,3,2,1,0:T(8,128)(2,1)} %reshape.342) | data formatting | bytes 9437184 | tf_op jit(solution)/shard_map/reshape | solution.py:85
  249.2 11.4 %reshape.358 = bf16[8,2,147456]{2,1,0:T(2,128)(2,1)} reshape(bf16[8,9,8,2,32,64]{5,4,3,2,1,0:T(8,128)(2,1)} %bitcast.106) | data formatting | bytes 9437184
  260.6 8.0 %all-to-all-start.1 = ((bf16[8,2,147456]{2,1,0:T(2,128)(2,1)}), bf16[8,2,147456]{2,1,0:T(2,128)(2,1)}, u32[]{:S(2)}, u32[]{:S(2)}) async-start(bf16[8,2,147456]{2,1,0:T(2,128)(2,1)} %reshape.358), calls=%async_computation.1 | async-start | bytes 9437184 | tf_op jit(solution)/shard_map/all_to_all | solution.py:86
  268.6 0.6 fusion.121
  269.8 0.7 bitcast_multiply_fusion.1
  270.5 1.2 fusion.71
  271.8 0.1 copy.34
  271.8 0.1 copy.33
  271.9 0.1 copy.32
  272.0 0.7 convert_bitcast_fusion.1
  272.7 0.1 broadcast_multiply_fusion
  272.9 0.1 subtract_multiply_fusion
  273.0 0.1 subtract_multiply_fusion.1
  273.1 49.9 %all-to-all-done.1 = bf16[8,2,147456]{2,1,0:T(2,128)(2,1)} async-done(((bf16[8,2,147456]{2,1,0:T(2,128)(2,1)}), bf16[8,2,147456]{2,1,0:T(2,128)(2,1)}, u32[]{:S(2)}, u32[]{:S(2)}) %all-to-all-start.1) | async-done | bytes 4718624 | tf_op jit(solution)/shard_map/all_to_all | solution.py:86
  323.0 11.2 %reshape.359 = bf16[8,9,8,2,32,64]{5,4,3,2,1,0:T(8,128)(2,1)} reshape(bf16[8,2,147456]{2,1,0:T(2,128)(2,1)} %all-to-all-done.1) | data formatting | bytes 9437184
  334.2 4.6 %gather_fusion = bf16[16,8,2,32,64]{4,3,2,1,0:T(8,128)(2,1)S(1)} fusion(bf16[72,8,2,32,64]{4,3,2,1,0:T(8,128)(2,1)} %bitcast.108, s32[1024]{0:T(1024)S(1)} %pad_clamp_fusion), kind=kCustom, calls=%fused_computation | custom fusion | bytes 2097216 | tf_op jit(solution)/shard_map/jit(_take)/gather | solution.py:87
  338.8 0.3 select_convert_fusion
  339.2 10.7 %subtract_reduce_fusion = (f32[32,64]{1,0:T(8,128)S(1)}, f32[32,64]{1,0:T(8,128)S(1)}) fusion(f32[16,8,2,32,64]{4,3,2,1,0:T(8,128)S(1)} %select_convert_fusion, f32[]{:T(128)} %bitcast.25, f32[]{:T(128)} %bitcast.24, f32[16,8,64]{2,1,0:T(8,128)S(1)} %subtract_multiply_fusion, f32[16,8,32]{2,1,0:T(8,128)S(1)} %subtract_multiply_fusion.1, f32[]{:T(128)} %bitcast.23, ...), kind=kLoop, calls=%fused_computation.19 | loop fusion | flops 4976640 | bytes 2163276 | tf_op jit(solution)/shard_map/reduce_sum | solution.py:105
  349.9 1.4 fusion.54
  351.3 1.4 fusion.52
  352.6 1.4 fusion.12
  354.0 1.4 fusion.13
  355.4 0.8 copy.46
  356.2 30.5 %reduce-scatter.4.cloned.1.call-done = f32[64,64]{1,0:T(8,128)} async-done(((f32[512,64]{1,0:T(8,128)}), f32[64,64]{1,0:T(8,128)}) %reduce-scatter.4.cloned.1.call-update) | async-done | bytes 16400
  386.7 0.8 copy.47
  387.6 0.1 copy.35
  387.7 0.1 reshape.360
  387.8 12.9 %all_to_all.51 = f32[16,1,256]{2,1,0:T(1,128)S(1)} all-to-all(f32[16,1,256]{2,1,0:T(1,128)S(1)} %reshape.360), channel_id=1, replica_groups=mesh['det'=8,'scan'=16] {'scan'}, dimensions={0} | all-to-all | bytes 32768 | tf_op jit(solution)/shard_map/all_to_all | solution.py:126
  400.7 0.5 broadcast.541
  401.2 0.7 reduce
  401.9 0.1 reshape.361
  402.0 0.1 all_to_all.47
  402.2 4.5 %fusion.39 = f32[4,512]{1,0:T(4,128)S(1)} fusion(f32[4,1,512]{2,1,0:T(1,128)S(1)} %get-tuple-element.12), kind=kOutput, calls=%fused_computation.62 | convolution fusion | flops 16252928 | bytes 16384 | tf_op jit(solution)/shard_map/dot_general | solution.py:132
  406.6 4.5 %fusion.37 = f32[4,512]{1,0:T(4,128)S(1)} fusion(f32[4,1,512]{2,1,0:T(1,128)S(1)} %get-tuple-element.12), kind=kOutput, calls=%fused_computation.61 | convolution fusion | flops 16252928 | bytes 16384 | tf_op jit(solution)/shard_map/dot_general | solution.py:128
  411.2 4.5 %fusion.15 = f32[1,4,512]{2,1,0:T(4,128)S(1)} fusion(f32[4,512]{1,0:T(4,128)S(1)} %fusion.39, f32[4,1,512]{2,1,0:T(1,128)S(1)} %get-tuple-element.11), kind=kOutput, calls=%fused_computation.37 | convolution fusion | flops 16257024 | bytes 24576 | tf_op jit(solution)/shard_map/dot_general | solution.py:133
  415.7 4.5 %fusion.17 = f32[1,4,512]{2,1,0:T(4,128)S(1)} fusion(f32[4,512]{1,0:T(4,128)S(1)} %fusion.37, f32[4,1,512]{2,1,0:T(1,128)S(1)} %get-tuple-element.11), kind=kOutput, calls=%fused_computation.40 | convolution fusion | flops 16257024 | bytes 24576 | tf_op jit(solution)/shard_map/dot_general | solution.py:129
  420.2 0.7 pad_maximum_fusion.3
  (18 shorter events, 0.2 us)
Async XLA Ops:
  35.8 153.7 %all-to-all-start = ((bf16[72,32,2,512]{0,1,2,3:T(8,128)(2,1)}), bf16[72,32,2,512]{0,1,2,3:T(8,128)(2,1)}, u32[]{:S(2)}, u32[]{:S(2)}) async-start(bf16[72,32,2,512]{0,1,2,3:T(8,128)(2,1)} %copy.26), calls=%async_computation | async-start | bytes 16777216 | tf_op jit(solution)/shard_map/all_to_all | solution.py:81
  203.2 14.6 %copy-start = (bf16[1,2,512,512]{3,2,1,0:T(8,128)(2,1)S(1)}, bf16[1,2,512,512]{3,2,1,0:T(8,128)(2,1)}, u32[]{:S(2)}) copy-start(bf16[1,2,512,512]{3,2,1,0:T(8,128)(2,1)} %get-tuple-element.10) | copy-start | bytes 3145732
  260.6 8.0 %copy-start.1 = (f32[3]{0:T(128)S(1)}, f32[3]{0:T(128)}, u32[]{:S(2)}) copy-start(f32[3]{0:T(128)} %param.5) | copy-start | bytes 40
  260.6 62.4 %all-to-all-start.1 = ((bf16[8,2,147456]{2,1,0:T(2,128)(2,1)}), bf16[8,2,147456]{2,1,0:T(2,128)(2,1)}, u32[]{:S(2)}, u32[]{:S(2)}) async-start(bf16[8,2,147456]{2,1,0:T(2,128)(2,1)} %reshape.358), calls=%async_computation.1 | async-start | bytes 9437184 | tf_op jit(solution)/shard_map/all_to_all | solution.py:86
  268.6 118.1 %reduce-scatter.4.cloned.1.call-start = ((), (), s32[]{:S(2)}) async-start(), calls=%async_computation.4 | async-start | bytes 294912
Sparse Core Ops, SparseCore 0:
  356.4 30.3 reduce-scatter.3
where the time goes:
time: 433 us; the launch traced here: 428 us
  waiting for transfers between devices  225 us (52%)
  local copies, waits for them, and re-layouts  95 us (22%)
  matrix products  39.8 us (9%)
  other arithmetic  24.9 us (6%)
  starting transfers between devices  15.6 us (4%)
  between operations  14.2 us (3%)
  blocking collectives  12.9 us (3%)
    all_to_all x1, waiting for transfers between devices, shards(): lax.all_to_all(row_fourier_spectrum, 'scan', split_axis=3, concat_axis=1,...  145 us
    all_to_all x1, waiting for transfers between devices, shards(): lax.all_to_all(spectrum, 'det', split_axis=4, concat_axis=0, tiled=True)  49.9 us
    unnamed x2, waiting for transfers between devices  30.5 us
    all_to_all x2, local copies, waits for them, and re-layouts, shards(): lax.all_to_all(row_fourier_spectrum, 'scan', split_axis=3, concat_axis=1,...  28.2 us
    unnamed x10, local copies, waits for them, and re-layouts  24.4 us
    reshape x2, local copies, waits for them, and re-layouts, shards(): spectrum.reshape(blocks_dev, BLK, 2, tile_cols, det_count, tile_rows)  22.4 us
    convert_element_type x1, local copies, waits for them, and re-layouts, shards(): row_fourier_spectrum = jnp.einsum('tlf,inf->tlin', intensity, table_row_c...  13.8 us
    all_to_all x1, blocking collectives, shards(): lax.all_to_all(back_rows, 'scan', split_axis=0, concat_axis=2, tiled=True)  12.9 us
  transfers between devices with their start and end apart: 3, of which 3 were waited for; matrix products, arithmetic and copies ran while one was open for 1% of the time, Pallas kernels for 0%

commit v1 on v0

v1 whole, which is shorter than its diff:
```python
import math

import jax
import jax.numpy as jnp
import numpy as np
from jax import lax
from jax.experimental import pallas as pl
from jax.experimental.pallas import tpu as pltpu
from jax.sharding import PartitionSpec as P

DSIDE = 24
BLK = 8
N = 512
DET = 8
SCAN = 16
BPD = 9
COLS = 16
ROWS = N // SCAN
TILE_ROWS = N // DET
FREQ_STEP = 4.0 / N
PITCH = 2.4 / DSIDE
CENTRE = (DSIDE - 1) / 2.0
QUARTIC = 0.05
SCALE = 1.0 / (N * N * math.sqrt(16 * BLK))


def poly_tables():
    nodes = (0.5 * np.cos((np.arange(64) + 0.5) * np.pi / 64)) ** 2
    z = np.concatenate([nodes, [0.0]])
    x = np.sqrt(z)
    cos_c = np.polynomial.polynomial.polyfit(z, np.cos(2 * np.pi * x), 6)
    ratio = 2 * np.pi * np.sinc(2 * x)
    sin_c = np.polynomial.polynomial.polyfit(z, ratio, 6)
    return [float(v) for v in cos_c], [float(v) for v in sin_c]


COS_C, SIN_C = poly_tables()


def dft_tables():
    n = np.arange(N)
    angle = (n[:, None] * n[None, :] % N) * (2.0 * np.pi / N)
    return np.cos(angle), np.sin(angle)


def constants():
    cos, sin = dft_tables()
    bf16 = jnp.bfloat16
    re_part = cos[:, : N // 2]
    im_part = -sin[:, : N // 2]
    im_part[:, 0] = cos[:, N // 2]
    row_table = np.concatenate([re_part, im_part], axis=1).astype(bf16)
    col_table = np.concatenate([cos, sin], axis=0).astype(bf16)
    c = np.arange(N // 2).reshape(SCAN, COLS)
    mirrored = N - c
    mirrored[0, 0] = N // 2
    order = np.stack([c, mirrored], axis=1).reshape(-1)
    last_table = np.concatenate([cos[order], sin[order]], axis=1).astype(bf16)
    return row_table, col_table, last_table


def row_kernel(x_ref, table_ref, o_ref):
    x = x_ref[...].reshape(BLK * ROWS, N)
    y = jnp.dot(x, table_ref[...], preferred_element_type=jnp.float32)
    group = lax.broadcasted_iota(jnp.int32, (ROWS, 128), 1) // COLS
    for part in range(2):
        for half in range(2):
            col = (part * 2 + half) * 128
            a = [y[ROWS * p : ROWS * (p + 1), col : col + 128] for p in range(BLK)]
            for k in range(3):
                width = COLS << k
                low = (group >> k) & 1 == 0
                for p in range(BLK):
                    if p >> k & 1:
                        continue
                    q = p | 1 << k
                    first = jnp.where(low, a[p], pltpu.roll(a[q], width, 1))
                    second = jnp.where(low, pltpu.roll(a[p], 128 - width, 1), a[q])
                    a[p], a[q] = first, second
            for d in range(BLK):
                o_ref[half * 8 + d, :, part * 128 : (part + 1) * 128] = a[d].astype(jnp.bfloat16)


def column_kernel(meta_ref, flags_ref, ab_ref, r_ref, table_ref, o_ref, pq_ref, acc_ref):
    b = pl.program_id(0)
    f32 = jnp.float32

    @pl.when(b == 0)
    def _():
        acc_ref[...] = jnp.zeros_like(acc_ref)

    pq_ref[...] = jnp.dot(table_ref[...], r_ref[...], preferred_element_type=f32)

    det = meta_ref[0]
    scan = meta_ref[1]
    a0, a1, a2 = ab_ref[0], ab_ref[1], ab_ref[2]
    kappa = QUARTIC * a1
    plus = a0 + a2
    minus = a0 - a2
    block = det * BPD + b
    lane = lax.broadcasted_iota(jnp.int32, (1, 128), 1)
    pix = lane // COLS
    col = lane % COLS
    column = scan * COLS + col
    special = column == 0
    keep = jnp.where(special, 0.0, 1.0)
    kx = ((lax.rem(block, 3) * BLK + pix).astype(f32) - CENTRE) * PITCH
    ky = (jnp.full((1, 128), lax.div(block, 3), jnp.int32).astype(f32) - CENTRE) * PITCH
    kx2 = kx * kx
    ky2 = ky * ky
    chi_k = plus * kx2 + minus * ky2 + kappa * (kx2 + ky2) * (kx2 + ky2)
    freq_direct = column.astype(f32) * FREQ_STEP
    freq_mirror = jnp.where(special, -(N // 2) * FREQ_STEP, -freq_direct)
    row = lax.broadcasted_iota(jnp.int32, (TILE_ROWS, 128), 0).astype(f32)

    def tile(t, _):
        start = pl.multiple_of(t * TILE_ROWS, TILE_ROWS)
        w_direct = flags_ref[b * 8 + t]
        w_mirror = flags_ref[72 + b * 8 + t]
        w_extra = flags_ref[144 + b * 8 + t]
        base = jnp.full((1, 128), start - jnp.where(t >= 4, N, 0), jnp.int32).astype(f32) * FREQ_STEP

        def add(w, freq_x, mirror):
            ux = kx - w * freq_x
            x2 = ux * ux
            fx = 0.5 * (chi_k - plus * x2 - kappa * x2 * x2)
            dx = -0.5 * minus - kappa * x2
            bx = -0.5 * kappa
            alpha = ky - w * base
            beta = -w * FREQ_STEP
            uy = alpha + beta * row
            y2 = uy * uy
            turns = fx + y2 * (dx + bx * y2)
            x = turns - jnp.floor(turns + 0.5)
            z = x * x
            cos = COS_C[6]
            for v in COS_C[5::-1]:
                cos = cos * z + v
            sin = SIN_C[6]
            for v in SIN_C[5::-1]:
                sin = sin * z + v
            if mirror:
                x = x * (w * w)
            sin = sin * x
            cos = cos * w
            p1 = pq_ref[pl.ds(start, TILE_ROWS), :128]
            p3 = pq_ref[pl.ds(start, TILE_ROWS), 128:]
            p2 = pq_ref[pl.ds(N + start, TILE_ROWS), :128]
            p4 = pq_ref[pl.ds(N + start, TILE_ROWS), 128:]
            if mirror:
                g_re = jnp.where(special, p3, p1 - p4)
                h_im = jnp.where(special, p4, p3 + p2)
                real = g_re * cos + h_im * sin
                imag = g_re * sin - h_im * cos
            else:
                g_re = p1 + keep * p4
                g_im = keep * p3 - p2
                real = g_re * cos - g_im * sin
                imag = g_re * sin + g_im * cos
            k = 1 if mirror else 0
            acc_ref[pl.ds(start, TILE_ROWS), k * 128 : (k + 1) * 128] += real
            acc_ref[pl.ds(start, TILE_ROWS), (k + 2) * 128 : (k + 3) * 128] += imag

        @pl.when(w_direct != 0)
        def _():
            add(jnp.full((1, 128), w_direct, jnp.int32).astype(f32), freq_direct, False)

        @pl.when(jnp.logical_or(w_mirror != 0, w_extra != 0))
        def _():
            w = jnp.where(col == 0, w_extra, w_mirror).astype(f32)
            add(w, freq_mirror, True)

        return 0

    lax.fori_loop(0, DET, tile, 0)

    @pl.when(b == BPD - 1)
    def _():
        src = lax.broadcasted_iota(jnp.int32, (N, 128), 0)
        dst = lax.broadcasted_iota(jnp.int32, (N, 128), 1)
        pick = (src // 128 == dst % 64 // COLS) & (src % COLS == dst % COLS)
        pick = jnp.where(pick, 1.0, 0.0).astype(jnp.bfloat16)
        lune = jnp.dot(acc_ref[...].astype(jnp.bfloat16), pick, preferred_element_type=f32)
        high = lune.astype(jnp.bfloat16).astype(f32)
        packed = jnp.where(dst < 64, high, lune - high).astype(jnp.bfloat16)
        g = jnp.dot(table_ref[...], packed, preferred_element_type=f32)
        g_cos = g[:N]
        g_sin = g[N:]
        is_re = dst // 32 % 2 == 0
        swapped = jnp.where(is_re, -pltpu.roll(g_sin, 96, 1), pltpu.roll(g_sin, 32, 1))
        out = g_cos + swapped
        out = out + pltpu.roll(out, 64, 1)
        o_ref[...] = out[:, :64].astype(jnp.bfloat16)


def last_kernel(y_ref, table_ref, o_ref):
    f32 = jnp.float32
    y = y_ref[0:64, :].astype(f32)
    for d in range(1, DET):
        y = y + y_ref[64 * d : 64 * (d + 1), :].astype(f32)
    top = lax.broadcasted_iota(jnp.int32, (8, 64), 0) < 4
    parts = []
    for half in range(2):
        pieces = []
        for u in range(8):
            rows = y[8 * u : 8 * (u + 1), :]
            pieces.append(jnp.where(top, rows, 0.0)[:, 32 * half : 32 * (half + 1)])
            pieces.append(jnp.where(top, 0.0, rows)[:, 32 * half : 32 * (half + 1)])
        parts.append(jnp.concatenate(pieces, axis=1))
    lhs = jnp.concatenate(parts, axis=0)
    high = lhs.astype(jnp.bfloat16)
    low = (lhs - high.astype(f32)).astype(jnp.bfloat16)
    out = jnp.dot(high, table_ref[...], preferred_element_type=f32)
    out = out + jnp.dot(low, table_ref[...], preferred_element_type=f32)
    re, im = out[0:8], out[8:16]
    image_re = re[:, :N] - im[:, N:]
    image_im = re[:, N:] + im[:, :N]
    o_ref[0] = (image_re[0:4] + image_re[4:8]) * SCALE
    o_ref[1] = (image_im[0:4] + image_im[4:8]) * SCALE


def shards(intensity, aberrations, lune_blocks, lune_weight):
    det = lax.axis_index("det").astype(jnp.int32)
    scan = lax.axis_index("scan").astype(jnp.int32)
    row_table, col_table, last_table = (jnp.asarray(v) for v in constants())
    bf16 = jnp.bfloat16

    half = scan // 2
    extra = jnp.where(scan % 2 == 0, jnp.where(scan == 0, 8, 16 - half), 15 - half)
    columns = jnp.stack([half, 15 - half, extra])
    blocks = jnp.take(lune_blocks, columns, axis=1)
    weights = jnp.take(lune_weight, columns, axis=1)
    own = det * BPD + jnp.arange(BPD, dtype=jnp.int32)
    hits = blocks[..., None] == own
    flags = jnp.sum(jnp.where(hits, weights[..., None], 0), axis=2)
    flags = flags.transpose(1, 2, 0).reshape(-1)
    meta = jnp.stack([det, scan])

    rows = pl.pallas_call(
        row_kernel,
        grid=(BPD,),
        in_specs=[
            pl.BlockSpec((BLK, ROWS, N), lambda b: (b, 0, 0)),
            pl.BlockSpec((N, N), lambda b: (0, 0)),
        ],
        out_specs=pl.BlockSpec((SCAN, ROWS, 256), lambda b: (0, 0, b)),
        out_shape=jax.ShapeDtypeStruct((SCAN, ROWS, BPD * 256), bf16),
        name="rows",
    )(intensity, row_table)

    spread = lax.all_to_all(rows.reshape(N, BPD * 256), "scan", 0, 0, tiled=True)

    smem = pl.BlockSpec(memory_space=pltpu.SMEM)
    back = pl.pallas_call(
        column_kernel,
        grid=(BPD,),
        in_specs=[
            smem,
            smem,
            smem,
            pl.BlockSpec((N, 256), lambda b: (0, b)),
            pl.BlockSpec((2 * N, N), lambda b: (0, 0)),
        ],
        out_specs=pl.BlockSpec((N, 64), lambda b: (0, 0)),
        out_shape=jax.ShapeDtypeStruct((N, 64), bf16),
        scratch_shapes=[
            pltpu.VMEM((2 * N, 256), jnp.float32),
            pltpu.VMEM((N, 512), jnp.float32),
        ],
        name="columns",
    )(meta, flags, aberrations, spread, col_table)

    parts = lax.all_to_all(back, ("det", "scan"), 0, 0, tiled=True)

    return pl.pallas_call(
        last_kernel,
        out_shape=jax.ShapeDtypeStruct((2, 4, N), jnp.float32),
        name="last",
    )(parts, last_table)


def solution(mesh):
    return jax.shard_map(
        shards,
        mesh=mesh,
        in_specs=(P("det", "scan", None), P(), P(), P()),
        out_specs=P(None, ("det", "scan"), None),
        check_vma=False,
    )
```

time: 433 us -> 84.8 us (0.20); the launches traced: 428 us -> 84.2 us
  waiting for transfers between devices: 225 us -> 28.5 us
  local copies, waits for them, and re-layouts: 95 us -> 5.06 us
  matrix products: 39.8 us -> 0 us
  other arithmetic: 24.9 us -> 1.38 us
  Pallas kernels: 0 us -> 22.8 us
  between operations: 14.2 us -> 0.09 us
  starting transfers between devices: 15.6 us -> 7.7 us
  blocking collectives: 12.9 us -> 18.6 us
    all_to_all x2 -> x1, waiting for transfers between devices: 195 us -> 28.5 us  [shards(): lax.all_to_all(rows.reshape(N, BPD * 256), 'scan', 0, 0, tiled=True)]
    dot_general x10 -> x0, matrix products: 39.8 us -> none  [the longest x1 9.14 us: shards(): jnp.einsum('oiqr,nric->nocq', table_cols, lax.all_to_all(row_fourier_spec...]
    unnamed x2 -> x0, waiting for transfers between devices: 30.5 us -> none
    all_to_all x6 -> x0, local copies, waits for them, and re-layouts: 28.8 us -> none  [the longest x2 28.2 us: shards(): lax.all_to_all(row_fourier_spectrum, 'scan', split_axis=3, concat_axis=1,...]
    pallas_call x0 -> x3, Pallas kernels: none -> 22.8 us  [the longest x1 11.7 us: shards(): pl.pallas_call(column_kernel, grid=(BPD,), in_specs=[smem, smem, smem, pl...]
    reshape x2 -> x1, local copies, waits for them, and re-layouts: 22.4 us -> 0.66 us  [shards(): flags = flags.transpose(1, 2, 0).reshape(-1)]
    unnamed x10 -> x8, local copies, waits for them, and re-layouts: 24.4 us -> 3.21 us
    convert_element_type x1 -> x0, local copies, waits for them, and re-layouts: 13.8 us -> none  [shards(): row_fourier_spectrum = jnp.einsum('tlf,inf->tlin', intensity, table_row_c...]
  transfers between devices with their start and end apart: 3 -> 1, of which waited for: 3 -> 1; matrix products, arithmetic and copies ran while one was open for 1% -> 4% of each run, Pallas kernels for 0% -> 0%
where the time goes in v1:
time: 84.8 us; the launch traced here: 84.2 us
  waiting for transfers between devices  28.5 us (34%)
  Pallas kernels  22.8 us (27%)
  blocking collectives  18.6 us (22%)
  starting transfers between devices  7.7 us (9%)
  local copies, waits for them, and re-layouts  5.06 us (6%)
  other arithmetic  1.38 us (2%)
    all_to_all x1, waiting for transfers between devices, shards(): lax.all_to_all(rows.reshape(N, BPD * 256), 'scan', 0, 0, tiled=True)  28.5 us
    all_to_all x1, blocking collectives, shards(): parts = lax.all_to_all(back, ('det', 'scan'), 0, 0, tiled=True)  18.6 us
    pallas_call x1, Pallas kernels, shards(): pl.pallas_call(column_kernel, grid=(BPD,), in_specs=[smem, smem, smem, pl...  11.7 us
    pallas_call x1, Pallas kernels, shards(): pl.pallas_call(row_kernel, grid=(BPD,), in_specs=[pl.BlockSpec((BLK, ROWS...  8.82 us
    all_to_all x1, starting transfers between devices, shards(): lax.all_to_all(rows.reshape(N, BPD * 256), 'scan', 0, 0, tiled=True)  7.7 us
    unnamed x8, local copies, waits for them, and re-layouts  3.21 us
    pallas_call x1, Pallas kernels, shards(): pl.pallas_call(last_kernel, out_shape=jax.ShapeDtypeStruct((2, 4, N), jnp...  2.36 us
  transfers between devices with their start and end apart: 1, of which 1 were waited for; matrix products, arithmetic and copies ran while one was open for 4% of the time, Pallas kernels for 0%

profile of v1, /device:TPU:1, one launch (start us, length us, event | category | flops | bytes accessed | tf_op | source)
XLA Modules:
  0.0 84.2 jit_solution(16087746471208609642)
XLA Ops:
  0.0 0.0 copy-start
  0.0 8.8 %rows.1 = bf16[16,32,2304]{2,1,0:T(8,128)(2,1)} custom-call(bf16[72,32,512]{2,1,0:T(8,128)(2,1)} %x_ref.1, bf16[512,512]{1,0:T(8,128)(2,1)} %constant.58.clone.table_ref), custom_call_target="tpu_custom_call" | custom-call | tf_op jit(solution)/shard_map/rows/pallas_call | solution.py:239
  8.8 0.0 copy-start.2
  8.8 7.7 %all-to-all-start = ((bf16[16,32,2304]{2,1,0:T(8,128)(2,1)}), bf16[16,32,2304]{2,1,0:T(8,128)(2,1)S(1)}, u32[]{:S(2)}, u32[]{:S(2)}) async-start(bf16[16,32,2304]{2,1,0:T(8,128)(2,1)} %rows.1), calls=%async_computation | async-start | bytes 4718592 | tf_op jit(solution)/shard_map/all_to_all | solution.py:251
  16.6 0.1 compare_and_fusion
  16.7 0.0 copy-done
  16.7 0.6 gather_fusion.1
  17.3 0.0 copy-done.2
  17.3 0.6 gather_fusion
  17.9 0.1 select_bitcast_fusion.1
  18.0 0.6 select_reduce_fusion
  18.6 0.7 reshape.20.flags_ref
  19.2 0.6 pad_add_fusion.meta_ref
  19.8 28.5 %all-to-all-done = bf16[16,32,2304]{2,1,0:T(8,128)(2,1)S(1)} async-done(((bf16[16,32,2304]{2,1,0:T(8,128)(2,1)}), bf16[16,32,2304]{2,1,0:T(8,128)(2,1)S(1)}, u32[]{:S(2)}, u32[]{:S(2)}) %all-to-all-start) | async-done | bytes 2359328 | tf_op jit(solution)/shard_map/all_to_all | solution.py:251
  48.4 0.0 copy-start.1
  48.4 1.4 %copy-done.1 = bf16[16,32,2304]{2,1,0:T(8,128)(2,1)} copy-done((bf16[16,32,2304]{2,1,0:T(8,128)(2,1)}, bf16[16,32,2304]{2,1,0:T(8,128)(2,1)S(1)}, u32[]{:S(2)}) %copy-start.1) | copy-done | bytes 2359320
  49.8 11.7 %columns.1 = bf16[512,64]{1,0:T(8,128)(2,1)} custom-call(s32[2]{0:T(128)} %pad_add_fusion.meta_ref, s32[216]{0:T(256)} %reshape.20.flags_ref, f32[3]{0:T(128)} %ab_ref.1, bf16[512,2304]{1,0:T(8,128)(2,1)} %bitcast.13, bf16[1024,512]{1,0:T(8,128)(2,1)} %constant.59.clone.table_ref), custom_call_target="tpu_custom_call" | custom-call | tf_op jit(solution)/shard_map/columns/pallas_call | solution.py:254
  61.5 1.0 %reshape.43 = bf16[128,2,128]{2,1,0:T(2,128)(2,1)S(1)} reshape(bf16[128,4,64]{2,1,0:T(4,128)(2,1)} %bitcast.14) | data formatting | bytes 131072
  62.5 18.6 %all_to_all.19 = bf16[128,2,128]{2,1,0:T(2,128)(2,1)S(1)} all-to-all(bf16[128,2,128]{2,1,0:T(2,128)(2,1)S(1)} %reshape.43), channel_id=1, replica_groups=mesh['det'=8,'scan'=16] {'det','scan'}, dimensions={0} | all-to-all | bytes 131072 | tf_op jit(solution)/shard_map/all_to_all | solution.py:273
  81.1 0.8 reshape.44
  81.8 2.4 %last.1 = f32[2,4,512]{2,1,0:T(4,128)} custom-call(bf16[512,64]{1,0:T(8,128)(2,1)} %bitcast.15, bf16[512,1024]{1,0:T(8,128)(2,1)} %constant.60.clone.table_ref), custom_call_target="tpu_custom_call" | custom-call | tf_op jit(solution)/shard_map/last/pallas_call | solution.py:275
  (4 shorter events, 0.0 us)
Async XLA Ops:
  0.0 16.7 %copy-start = (s32[8,16,16]{2,1,0:T(8,128)S(1)}, s32[8,16,16]{2,1,0:T(8,128)}, u32[]{:S(2)}) copy-start(s32[8,16,16]{2,1,0:T(8,128)} %param.12) | copy-start | bytes 24580
  8.8 8.4 %copy-start.2 = (s32[8,16,16]{2,1,0:T(8,128)S(1)}, s32[8,16,16]{2,1,0:T(8,128)}, u32[]{:S(2)}) copy-start(s32[8,16,16]{2,1,0:T(8,128)} %param.11) | copy-start | bytes 24580
  8.8 39.5 %all-to-all-start = ((bf16[16,32,2304]{2,1,0:T(8,128)(2,1)}), bf16[16,32,2304]{2,1,0:T(8,128)(2,1)S(1)}, u32[]{:S(2)}, u32[]{:S(2)}) async-start(bf16[16,32,2304]{2,1,0:T(8,128)(2,1)} %rows.1), calls=%async_computation | async-start | bytes 4718592 | tf_op jit(solution)/shard_map/all_to_all | solution.py:251
  48.4 1.4 %copy-start.1 = (bf16[16,32,2304]{2,1,0:T(8,128)(2,1)}, bf16[16,32,2304]{2,1,0:T(8,128)(2,1)S(1)}, u32[]{:S(2)}) copy-start(bf16[16,32,2304]{2,1,0:T(8,128)(2,1)S(1)} %all-to-all-done) | copy-start | bytes 7077892

commit v2 on v1

v2 whole, which is shorter than its diff:
```python
import math

import jax
import jax.numpy as jnp
import numpy as np
from jax import lax
from jax.experimental import pallas as pl
from jax.experimental.pallas import tpu as pltpu
from jax.sharding import PartitionSpec as P

DSIDE = 24
BLK = 8
N = 512
DET = 8
SCAN = 16
BPD = 9
GROUP = 3
COLS = 16
ROWS = N // SCAN
TILE_ROWS = N // DET
FREQ_STEP = 4.0 / N
PITCH = 2.4 / DSIDE
CENTRE = (DSIDE - 1) / 2.0
QUARTIC = 0.05
SCALE = 1.0 / (N * N * math.sqrt(16 * BLK))


def poly_tables():
    nodes = (0.5 * np.cos((np.arange(64) + 0.5) * np.pi / 64)) ** 2
    z = np.concatenate([nodes, [0.0]])
    x = np.sqrt(z)
    cos_c = np.polynomial.polynomial.polyfit(z, np.cos(2 * np.pi * x), 6)
    ratio = 2 * np.pi * np.sinc(2 * x)
    sin_c = np.polynomial.polynomial.polyfit(z, ratio, 6)
    return [float(v) for v in cos_c], [float(v) for v in sin_c]


COS_C, SIN_C = poly_tables()


def dft_tables():
    n = np.arange(N)
    angle = (n[:, None] * n[None, :] % N) * (2.0 * np.pi / N)
    return np.cos(angle), np.sin(angle)


def constants():
    cos, sin = dft_tables()
    bf16 = jnp.bfloat16
    re_part = cos[:, : N // 2]
    im_part = -sin[:, : N // 2]
    im_part[:, 0] = cos[:, N // 2]
    row_table = np.concatenate([re_part, im_part], axis=1).astype(bf16)
    col_table = np.concatenate([cos, sin], axis=0).astype(bf16)
    c = np.arange(N // 2).reshape(SCAN, COLS)
    mirrored = N - c
    mirrored[0, 0] = N // 2
    order = np.stack([c, mirrored], axis=1).reshape(-1)
    last_table = np.concatenate([cos[order], sin[order]], axis=1).astype(bf16)
    return row_table, col_table, last_table


def row_kernel(x_hbm, table_hbm, o_hbm, x_ref, table_ref, o_ref, sems, out_sems):
    copies = [pltpu.make_async_copy(table_hbm, table_ref, sems.at[BPD])]
    for b in range(BPD):
        here = pl.ds(b * BLK, BLK)
        copies.append(pltpu.make_async_copy(x_hbm.at[here], x_ref.at[here], sems.at[b]))
    for copy in copies:
        copy.start()
    copies[0].wait()
    group = lax.broadcasted_iota(jnp.int32, (ROWS, 128), 1) // COLS
    bits = [(group >> k) & 1 == 1 for k in range(3)]
    for b in range(BPD):
        copies[1 + b].wait()
        x = x_ref[b * BLK : (b + 1) * BLK].reshape(BLK * ROWS, N)
        for part in range(2):
            y = jnp.dot(x, table_ref[:, part * 256 : (part + 1) * 256], preferred_element_type=jnp.float32)
            y = y.astype(jnp.bfloat16)
            for half in range(2):
                a = [y[ROWS * p : ROWS * (p + 1), half * 128 : (half + 1) * 128] for p in range(BLK)]
                for k in range(3):
                    a = [jnp.where(bits[k], a[(p + (1 << k)) % BLK], a[p]) for p in range(BLK)]
                a = [a[0]] + [pltpu.roll(a[p], COLS * p, 1) for p in range(1, BLK)]
                for k in range(3):
                    a = [jnp.where(bits[k], a[(p + (1 << k)) % BLK], a[p]) for p in range(BLK)]
                col = (b * 2 + part) * 128
                for d in range(BLK):
                    o_ref[half * 8 + d, :, col : col + 128] = a[-d % BLK]
        here = pl.ds(b * 256, 256)
        copies.append(pltpu.make_async_copy(o_ref.at[:, :, here], o_hbm.at[:, :, here], out_sems.at[b]))
        copies[-1].start()
    for copy in copies[BPD + 1 :]:
        copy.wait()


def phase_kernel(meta_ref, flags_ref, ab_ref, o_ref, pick_ref):
    f32 = jnp.float32
    b = pl.program_id(0)

    @pl.when(b == 0)
    def _():
        src = lax.broadcasted_iota(jnp.int32, (N, 256), 0)
        dst = lax.broadcasted_iota(jnp.int32, (N, 256), 1)
        for_sin = dst >= 128
        same = (src // 128 % 2 == dst // COLS % 2) & (src % COLS == dst % COLS)
        src_im = src // 256
        dst_im = dst // 32 % 2
        sign = jnp.where(for_sin & (dst_im == 0), -1.0, 1.0)
        match = (src_im == dst_im) != for_sin
        pick_ref[...] = jnp.where(same & match, sign, 0.0).astype(jnp.bfloat16)

    det = meta_ref[0]
    scan = meta_ref[1]
    a0, a1, a2 = ab_ref[0], ab_ref[1], ab_ref[2]
    kappa = QUARTIC * a1
    plus = a0 + a2
    minus = a0 - a2
    lane = lax.broadcasted_iota(jnp.int32, (1, 128), 1)
    pix = lane // COLS
    col = lane % COLS
    column = scan * COLS + col
    special = column == 0
    freq_direct = column.astype(f32) * FREQ_STEP
    freq_mirror = jnp.where(special, -(N // 2) * FREQ_STEP, -freq_direct)
    row = lax.broadcasted_iota(jnp.int32, (TILE_ROWS, 128), 0).astype(f32)

    def tile(t, _):
        i = b * DET + t
        start = pl.multiple_of(t * TILE_ROWS, TILE_ROWS)
        block = det * BPD + b
        kx = ((lax.rem(block, 3) * BLK + pix).astype(f32) - CENTRE) * PITCH
        ky = (jnp.full((1, 128), lax.div(block, 3), jnp.int32).astype(f32) - CENTRE) * PITCH
        kx2 = kx * kx
        ky2 = ky * ky
        chi_k = plus * kx2 + minus * ky2 + kappa * (kx2 + ky2) * (kx2 + ky2)
        w_direct = flags_ref[i]
        w_mirror = flags_ref[72 + i]
        w_extra = flags_ref[144 + i]
        base = jnp.full((1, 128), start - jnp.where(t >= 4, N, 0), jnp.int32).astype(f32) * FREQ_STEP

        def put(k, any_entry, w, freq_x):
            @pl.when(any_entry)
            def _():
                ux = kx - w * freq_x
                x2 = ux * ux
                fx = 0.5 * (chi_k - plus * x2 - kappa * x2 * x2)
                dx = -0.5 * minus - kappa * x2
                bx = -0.5 * kappa
                uy = (ky - w * base) - (w * FREQ_STEP) * row
                y2 = uy * uy
                turns = fx + y2 * (dx + bx * y2)
                x = turns - jnp.floor(turns + 0.5)
                z = x * x
                cos = COS_C[6]
                for v in COS_C[5::-1]:
                    cos = cos * z + v
                sin = SIN_C[6]
                for v in SIN_C[5::-1]:
                    sin = sin * z + v
                o_ref[0, pl.ds(start, TILE_ROWS), k * 128 : (k + 1) * 128] = cos * w
                o_ref[0, pl.ds(start, TILE_ROWS), (k + 1) * 128 : (k + 2) * 128] = sin * (x * (w * w))

            @pl.when(jnp.logical_not(any_entry))
            def _():
                o_ref[0, pl.ds(start, TILE_ROWS), k * 128 : (k + 2) * 128] = jnp.zeros((TILE_ROWS, 256), f32)

        put(0, w_direct != 0, jnp.full((1, 128), w_direct, jnp.int32).astype(f32), freq_direct)
        w = jnp.where(col == 0, w_extra, w_mirror).astype(f32)
        put(2, jnp.logical_or(w_mirror != 0, w_extra != 0), w, freq_mirror)
        return 0

    lax.fori_loop(0, DET, tile, 0)


def column_kernel(meta_ref, r_ref, phase_hbm, pick_hbm, table_ref, o_ref, *scratch):
    pq_ref, acc_ref, out_ref, phase_ref, pick_ref, sems = scratch
    f32 = jnp.float32
    bf16 = jnp.bfloat16
    copies = [pltpu.make_async_copy(phase_hbm.at[b], phase_ref.at[b], sems.at[b]) for b in range(BPD)]
    copies.append(pltpu.make_async_copy(pick_hbm, pick_ref, sems.at[BPD]))
    for copy in copies:
        copy.start()
    lane = lax.broadcasted_iota(jnp.int32, (1, 128), 1)
    special = meta_ref[1] * COLS + lane % COLS == 0
    keep = jnp.where(special, 0.0, 1.0)
    size = GROUP * 256
    step = 32

    def products(g):
        pq_ref[g % 2] = jnp.dot(table_ref[...], r_ref[:, g * size : (g + 1) * size], preferred_element_type=f32)

    def lunes(g):
        for i in range(GROUP):
            copies[g * GROUP + i].wait()
        for q in range(0, N, step):
            sums = [0.0] * 4 if g == 0 else [acc_ref[q : q + step, k * 128 : (k + 1) * 128] for k in range(4)]
            for i in range(GROUP):
                here = slice(i * 256, i * 256 + 128)
                there = slice(i * 256 + 128, i * 256 + 256)
                p1 = pq_ref[g % 2, q : q + step, here]
                p3 = pq_ref[g % 2, q : q + step, there]
                p2 = pq_ref[g % 2, N + q : N + q + step, here]
                p4 = pq_ref[g % 2, N + q : N + q + step, there]
                cos, sin, cos_m, sin_m = [
                    phase_ref[g * GROUP + i, q : q + step, k * 128 : (k + 1) * 128] for k in range(4)
                ]
                g_re = p1 + keep * p4
                g_im = keep * p3 - p2
                m_re = jnp.where(special, p3, p1 - p4)
                m_im = jnp.where(special, p4, p3 + p2)
                sums[0] += g_re * cos - g_im * sin
                sums[1] += m_re * cos_m + m_im * sin_m
                sums[2] += g_re * sin + g_im * cos
                sums[3] += m_re * sin_m - m_im * cos_m
            for k in range(4):
                acc_ref[q : q + step, k * 128 : (k + 1) * 128] = sums[k]

    products(0)
    for g in range(1, BPD // GROUP):
        products(g)
        lunes(g - 1)
    lunes(BPD // GROUP - 1)

    copies[BPD].wait()
    lune = jnp.dot(acc_ref[...].astype(bf16), pick_ref[...], preferred_element_type=f32)
    high = lune.astype(bf16).astype(f32)
    is_high = lax.broadcasted_iota(jnp.int32, (N, 256), 1) % 128 < 64
    packed = jnp.where(is_high, high, lune - high).astype(bf16)
    out_ref[...] = jnp.dot(table_ref[:N], packed[:, :128], preferred_element_type=f32) + jnp.dot(
        table_ref[N:], packed[:, 128:], preferred_element_type=f32
    )
    even = out_ref[pl.ds(0, N // 2, stride=2), :]
    odd = out_ref[pl.ds(1, N // 2, stride=2), :]
    first = lane < 64
    out = jnp.where(first, even, odd) + pltpu.roll(jnp.where(first, odd, even), 64, 1)
    o_ref[...] = out.astype(bf16)


def last_kernel(y_ref, table_ref, o_ref):
    f32 = jnp.float32
    bf16 = jnp.bfloat16
    y = y_ref[0:32, :].astype(f32)
    for d in range(1, DET):
        y = y + y_ref[32 * d : 32 * (d + 1), :].astype(f32)
    group = lax.broadcasted_iota(jnp.int32, (8, 128), 1) // 32
    own = lax.broadcasted_iota(jnp.int32, (8, 128), 0) // 2
    tiles = [[] for _ in range(4)]
    for u in range(4):
        rows = y[8 * u : 8 * (u + 1), :]
        turned = [rows] + [pltpu.roll(rows, 32 * k, 1) for k in range(1, 4)]
        for q in range(4):
            tile = jnp.zeros((8, 128), f32)
            for v in range(4):
                tile = jnp.where((own == v) & (group == v), turned[(v - q) % 4], tile)
            tiles[q].append(tile)
    lhs = jnp.concatenate([jnp.concatenate(tiles[q], axis=1) for q in range(4)], axis=0)
    high = lhs.astype(bf16)
    low = (lhs - high.astype(f32)).astype(bf16)
    both = jnp.concatenate([high, low], axis=0)
    out = jnp.dot(both, table_ref[...], preferred_element_type=f32)
    out = out[:32] + out[32:]
    for par in range(2):
        re = out[16 * par : 16 * par + 8]
        im = out[16 * par + 8 : 16 * par + 16]
        image_re = re[:, :N] - im[:, N:]
        image_im = re[:, N:] + im[:, :N]
        for k, image in enumerate((image_re, image_im)):
            image = image[0:4] + image[4:8]
            image = (image[0:2] + image[2:4]) * SCALE
            for h in range(2):
                o_ref[k, 2 * h + par : 2 * h + par + 1, :] = image[h : h + 1]


def shards(intensity, aberrations, lune_blocks, lune_weight):
    det = lax.axis_index("det").astype(jnp.int32)
    scan = lax.axis_index("scan").astype(jnp.int32)
    row_table, col_table, last_table = (jnp.asarray(v) for v in constants())
    bf16 = jnp.bfloat16
    f32 = jnp.float32

    half = scan // 2
    extra = jnp.where(scan % 2 == 0, jnp.where(scan == 0, 8, 16 - half), 15 - half)
    columns = jnp.stack([half, 15 - half, extra])
    blocks = jnp.take(lune_blocks, columns, axis=1)
    weights = jnp.take(lune_weight, columns, axis=1)
    own = det * BPD + jnp.arange(BPD, dtype=jnp.int32)
    hits = blocks[..., None] == own
    flags = jnp.sum(jnp.where(hits, weights[..., None], 0), axis=2)
    flags = flags.transpose(1, 2, 0).reshape(-1)
    meta = jnp.stack([det, scan])

    smem = pl.BlockSpec(memory_space=pltpu.SMEM)
    vmem = pl.BlockSpec(memory_space=pltpu.VMEM)
    hbm = pl.BlockSpec(memory_space=pl.ANY)

    def in_hbm(v):
        return pltpu.with_memory_space_constraint(v, pltpu.HBM)

    def on_chip(v):
        return pltpu.with_memory_space_constraint(v, pltpu.VMEM)

    rows = pl.pallas_call(
        row_kernel,
        in_specs=[hbm, hbm],
        out_specs=hbm,
        out_shape=pltpu.HBM((SCAN, ROWS, BPD * 256), bf16),
        scratch_shapes=[
            pltpu.VMEM((BPD * BLK, ROWS, N), bf16),
            pltpu.VMEM((N, N), bf16),
            pltpu.VMEM((SCAN, ROWS, BPD * 256), bf16),
            pltpu.SemaphoreType.DMA((BPD + 1,)),
            pltpu.SemaphoreType.DMA((BPD,)),
        ],
        compiler_params=pltpu.CompilerParams(vmem_limit_bytes=10 << 20),
        name="rows",
    )(in_hbm(intensity), in_hbm(row_table))

    spread = lax.all_to_all(rows.reshape(N, BPD * 256), "scan", 0, 0, tiled=True)

    phases, pick = pl.pallas_call(
        phase_kernel,
        grid=(BPD,),
        in_specs=[smem, smem, smem],
        out_specs=[pl.BlockSpec((1, N, N), lambda b: (b, 0, 0)), pl.BlockSpec((N, 256), lambda b: (0, 0))],
        out_shape=[pltpu.HBM((BPD, N, N), f32), pltpu.HBM((N, 256), bf16)],
        compiler_params=pltpu.CompilerParams(vmem_limit_bytes=8 << 20),
        name="phases",
    )(meta, flags, aberrations)

    back = pl.pallas_call(
        column_kernel,
        in_specs=[smem, vmem, hbm, hbm, vmem],
        out_specs=vmem,
        out_shape=jax.ShapeDtypeStruct((N // 2, 128), bf16),
        scratch_shapes=[
            pltpu.VMEM((2, 2 * N, GROUP * 256), f32),
            pltpu.VMEM((N, N), f32),
            pltpu.VMEM((N, 128), f32),
            pltpu.VMEM((BPD, N, N), f32),
            pltpu.VMEM((N, 256), bf16),
            pltpu.SemaphoreType.DMA((BPD + 1,)),
        ],
        compiler_params=pltpu.CompilerParams(vmem_limit_bytes=36 << 20),
        name="columns",
    )(meta, on_chip(spread), in_hbm(phases), in_hbm(pick), on_chip(col_table))

    parts = lax.all_to_all(back.reshape(DET * SCAN, 2, 128), ("det", "scan"), 0, 0, tiled=True)

    return pl.pallas_call(
        last_kernel,
        in_specs=[vmem, vmem],
        out_specs=vmem,
        out_shape=jax.ShapeDtypeStruct((2, 4, N), f32),
        compiler_params=pltpu.CompilerParams(vmem_limit_bytes=6 << 20),
        name="last",
    )(parts.reshape(N // 2, 128), on_chip(last_table))


def solution(mesh):
    return jax.shard_map(
        shards,
        mesh=mesh,
        in_specs=(P("det", "scan", None), P(), P(), P()),
        out_specs=P(None, ("det", "scan"), None),
        check_vma=False,
    )
```

time: 84.8 us -> 71.9 us (0.85)
  waiting for transfers between devices: 28.5 us -> 18.7 us
  local copies, waits for them, and re-layouts: 5.06 us -> 2.49 us
    all_to_all x1, waiting for transfers between devices: 28.5 us -> 18.7 us  [shards(): lax.all_to_all(rows.reshape(N, BPD * 256), 'scan', 0, 0, tiled=True)]
    unnamed x8 -> x10, local copies, waits for them, and re-layouts: 3.21 us -> 0.03 us
    pallas_call x3 -> x4, Pallas kernels: 22.8 us -> 22.3 us  [the longest x1 9 us: shards(): pl.pallas_call(phase_kernel, grid=(BPD,), in_specs=[smem, smem, smem], ou...]
  transfers between devices with their start and end apart: 1 -> 1, of which waited for: 1 -> 1; matrix products, arithmetic and copies ran while one was open for 4% -> 6% of each run, Pallas kernels for 0% -> 13%
where the time goes in v2:
time: 71.9 us; the launch traced here: 71.6 us
  Pallas kernels  22.3 us (31%)
  waiting for transfers between devices  18.7 us (26%)
  blocking collectives  18.7 us (26%)
  starting transfers between devices  7.72 us (11%)
  local copies, waits for them, and re-layouts  2.49 us (3%)
  other arithmetic  1.59 us (2%)
    all_to_all x1, waiting for transfers between devices, shards(): lax.all_to_all(rows.reshape(N, BPD * 256), 'scan', 0, 0, tiled=True)  18.7 us
    all_to_all x1, blocking collectives, shards(): lax.all_to_all(back.reshape(DET * SCAN, 2, 128), ('det', 'scan'), 0, 0, t...  18.7 us
    pallas_call x1, Pallas kernels, shards(): pl.pallas_call(phase_kernel, grid=(BPD,), in_specs=[smem, smem, smem], ou...  9 us
    all_to_all x1, starting transfers between devices, shards(): lax.all_to_all(rows.reshape(N, BPD * 256), 'scan', 0, 0, tiled=True)  7.72 us
    pallas_call x1, Pallas kernels, shards(): pl.pallas_call(column_kernel, in_specs=[smem, vmem, hbm, hbm, vmem], out_...  6.29 us
    pallas_call x1, Pallas kernels, shards(): pl.pallas_call(row_kernel, in_specs=[hbm, hbm], out_specs=hbm, out_shape=...  6.01 us
  transfers between devices with their start and end apart: 1, of which 1 were waited for; matrix products, arithmetic and copies ran while one was open for 6% of the time, Pallas kernels for 13%

profile of v2, /device:TPU:1, one launch (start us, length us, event | category | flops | bytes accessed | tf_op | source)
XLA Modules:
  0.0 71.6 jit_solution(15163742773123952529)
XLA Ops:
  0.0 0.0 copy-start
  0.0 6.0 %rows.1 = bf16[16,32,2304]{2,1,0:T(8,128)(2,1)} custom-call(bf16[72,32,512]{2,1,0:T(8,128)(2,1)} %x_hbm.1, bf16[512,512]{1,0:T(8,128)(2,1)} %constant.58.clone.table_hbm), custom_call_target="tpu_custom_call" | custom-call | tf_op jit(solution)/shard_map/rows/pallas_call | solution.py:302
  6.0 0.0 copy-start.4
  6.0 0.0 copy-start.3
  6.0 0.0 copy-start.1
  6.1 7.7 %all-to-all-start = ((bf16[16,32,2304]{2,1,0:T(8,128)(2,1)}), bf16[16,32,2304]{2,1,0:T(8,128)(2,1)S(1)}, u32[]{:S(2)}, u32[]{:S(2)}) async-start(bf16[16,32,2304]{2,1,0:T(8,128)(2,1)} %rows.1), calls=%async_computation | async-start | bytes 4718592 | tf_op jit(solution)/shard_map/all_to_all | solution.py:318
  13.8 0.1 compare_and_fusion
  13.9 0.0 copy-done
  13.9 1.2 %gather_fusion.1 = s32[3,8,16]{2,0,1:T(4,128)} fusion(s32[8,16,16]{2,1,0:T(8,128)S(1)} %copy-done, s32[1024]{0:T(1024)S(1)} %pad_clamp_fusion), kind=kCustom, calls=%fused_computation.1.clone | custom fusion | bytes 3084 | tf_op jit(solution)/shard_map/jit(_take)/gather | solution.py:285
  15.1 0.0 copy-done.4
  15.1 1.2 %gather_fusion = s32[3,8,16]{2,0,1:T(4,128)} fusion(s32[8,16,16]{2,1,0:T(8,128)S(1)} %copy-done.4, s32[1024]{0:T(1024)S(1)} %pad_clamp_fusion), kind=kCustom, calls=%fused_computation.clone | custom fusion | bytes 3084 | tf_op jit(solution)/shard_map/jit(_take)/gather | solution.py:284
  16.3 0.8 %select_bitcast_fusion.1 = (s32[8,3,16]{2,1,0:T(4,128)S(1)}, s32[8,3,16]{2,1,0:T(4,128)S(1)}) fusion(s32[3,8,16]{2,0,1:T(4,128)} %gather_fusion, pred[3]{0:T(512)(128)(4,1)S(1)} %get-tuple-element.10, s32[3,8,16]{2,0,1:T(4,128)} %gather_fusion.1), kind=kLoop, calls=%fused_computation.4 | loop fusion | flops 768 | bytes 6147 | tf_op jit(solution)/shard_map/jit(_take)/select_n | solution.py:284
  17.1 0.6 select_reduce_fusion
  17.7 0.1 reshape.24.flags_ref
  17.8 0.1 pad_add_fusion.meta_ref
  17.9 0.0 copy-done.3
  17.9 9.0 %phases.1 = (f32[9,512,512]{2,1,0:T(8,128)}, bf16[512,256]{1,0:T(8,128)(2,1)}) custom-call(s32[2]{0:T(128)S(1)} %pad_add_fusion.meta_ref, s32[216]{0:T(256)S(1)} %reshape.24.flags_ref, f32[3]{0:T(128)S(1)} %copy-done.3), custom_call_target="tpu_custom_call" | custom-call | tf_op jit(solution)/shard_map/phases/pallas_call | solution.py:320
  26.9 18.7 %all-to-all-done = bf16[16,32,2304]{2,1,0:T(8,128)(2,1)S(1)} async-done(((bf16[16,32,2304]{2,1,0:T(8,128)(2,1)}), bf16[16,32,2304]{2,1,0:T(8,128)(2,1)S(1)}, u32[]{:S(2)}, u32[]{:S(2)}) %all-to-all-start) | async-done | bytes 2359328 | tf_op jit(solution)/shard_map/all_to_all | solution.py:318
  45.6 0.0 copy-done.1
  45.6 0.0 copy-start.2
  45.6 6.3 %columns.1 = bf16[256,128]{1,0:T(8,128)(2,1)S(1)} custom-call(s32[2]{0:T(128)S(1)} %pad_add_fusion.meta_ref, bf16[512,2304]{1,0:T(8,128)(2,1)S(1)} %bitcast.13, f32[9,512,512]{2,1,0:T(8,128)} %get-tuple-element.8.phase_hbm, bf16[512,256]{1,0:T(8,128)(2,1)} %get-tuple-element.9.pick_hbm, bf16[1024,512]{1,0:T(8,128)(2,1)S(1)} %copy-done.1), custom_call_target="tpu_custom_call" | custom-call | tf_op jit(solution)/shard_map/columns/pallas_call | solution.py:330
  51.9 18.7 %all_to_all.13 = bf16[128,2,128]{2,1,0:T(2,128)(2,1)S(1)} all-to-all(bf16[128,2,128]{2,1,0:T(2,128)(2,1)S(1)} %bitcast.14), channel_id=1, replica_groups=mesh['det'=8,'scan'=16] {'det','scan'}, dimensions={0} | all-to-all | bytes 131072 | tf_op jit(solution)/shard_map/all_to_all | solution.py:347
  70.6 0.0 copy-done.2
  70.6 1.0 %last.1 = f32[2,4,512]{2,1,0:T(4,128)} custom-call(bf16[256,128]{1,0:T(8,128)(2,1)S(1)} %bitcast.15, bf16[512,1024]{1,0:T(8,128)(2,1)S(1)} %copy-done.2), custom_call_target="tpu_custom_call" | custom-call | tf_op jit(solution)/shard_map/last/pallas_call | solution.py:349
  (4 shorter events, 0.0 us)
Async XLA Ops:
  0.0 13.9 %copy-start = (s32[8,16,16]{2,1,0:T(8,128)S(1)}, s32[8,16,16]{2,1,0:T(8,128)}, u32[]{:S(2)}) copy-start(s32[8,16,16]{2,1,0:T(8,128)} %param.12) | copy-start | bytes 24580
  6.0 9.1 %copy-start.4 = (s32[8,16,16]{2,1,0:T(8,128)S(1)}, s32[8,16,16]{2,1,0:T(8,128)}, u32[]{:S(2)}) copy-start(s32[8,16,16]{2,1,0:T(8,128)} %param.11) | copy-start | bytes 24580
  6.0 11.9 %copy-start.3 = (f32[3]{0:T(128)S(1)}, f32[3]{0:T(128)}, u32[]{:S(2)}) copy-start(f32[3]{0:T(128)} %ab_ref.1) | copy-start | bytes 40
  6.0 39.6 %copy-start.1 = (bf16[1024,512]{1,0:T(8,128)(2,1)S(1)}, bf16[1024,512]{1,0:T(8,128)(2,1)}, u32[]{:S(2)}) copy-start(bf16[1024,512]{1,0:T(8,128)(2,1)} %constant.59.clone.table_ref) | copy-start | bytes 3145732
  6.1 39.5 %all-to-all-start = ((bf16[16,32,2304]{2,1,0:T(8,128)(2,1)}), bf16[16,32,2304]{2,1,0:T(8,128)(2,1)S(1)}, u32[]{:S(2)}, u32[]{:S(2)}) async-start(bf16[16,32,2304]{2,1,0:T(8,128)(2,1)} %rows.1), calls=%async_computation | async-start | bytes 4718592 | tf_op jit(solution)/shard_map/all_to_all | solution.py:318
  45.6 25.0 %copy-start.2 = (bf16[512,1024]{1,0:T(8,128)(2,1)S(1)}, bf16[512,1024]{1,0:T(8,128)(2,1)}, u32[]{:S(2)}) copy-start(bf16[512,1024]{1,0:T(8,128)(2,1)} %constant.60.clone.table_ref) | copy-start | bytes 3145732

commit v3 on v2

--- a/solution.py
+++ b/solution.py
@@ -14,7 +14,13 @@
 DET = 8
 SCAN = 16
 BPD = 9
+HALF = N // 2
+LEFT = HALF + 8
 GROUP = 3
+STEP = 16
+WAITS = {0: (1, 2), 2: (3, 4, 5, 6, 7, 8)}
+SENDS = (2, 5, 7, 8)
+PIECE = 64
 COLS = 16
 ROWS = N // SCAN
 TILE_ROWS = N // DET
@@ -51,7 +57,7 @@
     im_part = -sin[:, : N // 2]
     im_part[:, 0] = cos[:, N // 2]
     row_table = np.concatenate([re_part, im_part], axis=1).astype(bf16)
-    col_table = np.concatenate([cos, sin], axis=0).astype(bf16)
+    col_table = np.concatenate([sin[HALF:], sin[:HALF], cos], axis=0).astype(bf16)
     c = np.arange(N // 2).reshape(SCAN, COLS)
     mirrored = N - c
     mirrored[0, 0] = N // 2
@@ -60,24 +66,25 @@
     return row_table, col_table, last_table
 
 
-def row_kernel(x_hbm, table_hbm, o_hbm, x_ref, table_ref, o_ref, sems, out_sems):
+def row_kernel(x_hbm, table_hbm, o_hbm, x_ref, table_ref, y_ref, o_ref, sems, out_sems):
     copies = [pltpu.make_async_copy(table_hbm, table_ref, sems.at[BPD])]
     for b in range(BPD):
         here = pl.ds(b * BLK, BLK)
         copies.append(pltpu.make_async_copy(x_hbm.at[here], x_ref.at[here], sems.at[b]))
     for copy in copies:
         copy.start()
-    copies[0].wait()
     group = lax.broadcasted_iota(jnp.int32, (ROWS, 128), 1) // COLS
     bits = [(group >> k) & 1 == 1 for k in range(3)]
-    for b in range(BPD):
-        copies[1 + b].wait()
+
+    def transform(b):
         x = x_ref[b * BLK : (b + 1) * BLK].reshape(BLK * ROWS, N)
+        y_ref[...] = jnp.dot(x, table_ref[...], preferred_element_type=jnp.float32)
+
+    def exchange(b):
         for part in range(2):
-            y = jnp.dot(x, table_ref[:, part * 256 : (part + 1) * 256], preferred_element_type=jnp.float32)
-            y = y.astype(jnp.bfloat16)
             for half in range(2):
-                a = [y[ROWS * p : ROWS * (p + 1), half * 128 : (half + 1) * 128] for p in range(BLK)]
+                col = (part * 2 + half) * 128
+                a = [y_ref[ROWS * p : ROWS * (p + 1), col : col + 128].astype(jnp.bfloat16) for p in range(BLK)]
                 for k in range(3):
                     a = [jnp.where(bits[k], a[(p + (1 << k)) % BLK], a[p]) for p in range(BLK)]
                 a = [a[0]] + [pltpu.roll(a[p], COLS * p, 1) for p in range(1, BLK)]
@@ -86,10 +93,24 @@
                 col = (b * 2 + part) * 128
                 for d in range(BLK):
                     o_ref[half * 8 + d, :, col : col + 128] = a[-d % BLK]
-        here = pl.ds(b * 256, 256)
-        copies.append(pltpu.make_async_copy(o_ref.at[:, :, here], o_hbm.at[:, :, here], out_sems.at[b]))
-        copies[-1].start()
-    for copy in copies[BPD + 1 :]:
+
+    outs = []
+    sent = 0
+    copies[0].wait()
+    copies[1].wait()
+    transform(0)
+    for b in range(BPD):
+        for i in WAITS.get(b, ()):
+            copies[1 + i].wait()
+        exchange(b)
+        if b + 1 < BPD:
+            transform(b + 1)
+        if b in SENDS:
+            here = pl.ds(sent * 256, (b + 1 - sent) * 256)
+            outs.append(pltpu.make_async_copy(o_ref.at[:, :, here], o_hbm.at[:, :, here], out_sems.at[len(outs)]))
+            outs[-1].start()
+            sent = b + 1
+    for copy in outs:
         copy.wait()
 
 
@@ -122,54 +143,70 @@
     special = column == 0
     freq_direct = column.astype(f32) * FREQ_STEP
     freq_mirror = jnp.where(special, -(N // 2) * FREQ_STEP, -freq_direct)
-    row = lax.broadcasted_iota(jnp.int32, (TILE_ROWS, 128), 0).astype(f32)
+    row = lax.broadcasted_iota(jnp.int32, (TILE_ROWS, 128), 0)
+    block = det * BPD + b
+    kx = ((lax.rem(block, 3) * BLK + pix).astype(f32) - CENTRE) * PITCH
+    ky = (jnp.full((1, 128), lax.div(block, 3), jnp.int32).astype(f32) - CENTRE) * PITCH
+    kx2 = kx * kx
+    ky2 = ky * ky
+    chi_k = plus * kx2 + minus * ky2 + kappa * (kx2 + ky2) * (kx2 + ky2)
+
+    def put(k, start, any_entry, w, freq_x, freq_y):
+        here = pl.ds(start, TILE_ROWS)
+
+        @pl.when(any_entry)
+        def _():
+            ux = kx - w * freq_x
+            x2 = ux * ux
+            fx = 0.5 * (chi_k - plus * x2 - kappa * x2 * x2)
+            dx = -0.5 * minus - kappa * x2
+            bx = -0.5 * kappa
+            uy = ky - w * freq_y
+            y2 = uy * uy
+            turns = fx + y2 * (dx + bx * y2)
+            x = turns - jnp.floor(turns + 0.5)
+            z = x * x
+            cos = COS_C[6]
+            for v in COS_C[5::-1]:
+                cos = cos * z + v
+            sin = SIN_C[6]
+            for v in SIN_C[5::-1]:
+                sin = sin * z + v
+            o_ref[0, here, k * 128 : (k + 1) * 128] = (cos * w).astype(jnp.bfloat16)
+            o_ref[0, here, (k + 1) * 128 : (k + 2) * 128] = (sin * (x * (w * w))).astype(jnp.bfloat16)
+
+        @pl.when(jnp.logical_not(any_entry))
+        def _():
+            o_ref[0, here, k * 128 : (k + 2) * 128] = jnp.zeros((TILE_ROWS, 256), jnp.bfloat16)
 
     def tile(t, _):
-        i = b * DET + t
         start = pl.multiple_of(t * TILE_ROWS, TILE_ROWS)
-        block = det * BPD + b
-        kx = ((lax.rem(block, 3) * BLK + pix).astype(f32) - CENTRE) * PITCH
-        ky = (jnp.full((1, 128), lax.div(block, 3), jnp.int32).astype(f32) - CENTRE) * PITCH
-        kx2 = kx * kx
-        ky2 = ky * ky
-        chi_k = plus * kx2 + minus * ky2 + kappa * (kx2 + ky2) * (kx2 + ky2)
-        w_direct = flags_ref[i]
-        w_mirror = flags_ref[72 + i]
-        w_extra = flags_ref[144 + i]
-        base = jnp.full((1, 128), start - jnp.where(t >= 4, N, 0), jnp.int32).astype(f32) * FREQ_STEP
-
-        def put(k, any_entry, w, freq_x):
-            @pl.when(any_entry)
-            def _():
-                ux = kx - w * freq_x
-                x2 = ux * ux
-                fx = 0.5 * (chi_k - plus * x2 - kappa * x2 * x2)
-                dx = -0.5 * minus - kappa * x2
-                bx = -0.5 * kappa
-                uy = (ky - w * base) - (w * FREQ_STEP) * row
-                y2 = uy * uy
-                turns = fx + y2 * (dx + bx * y2)
-                x = turns - jnp.floor(turns + 0.5)
-                z = x * x
-                cos = COS_C[6]
-                for v in COS_C[5::-1]:
-                    cos = cos * z + v
-                sin = SIN_C[6]
-                for v in SIN_C[5::-1]:
-                    sin = sin * z + v
-                o_ref[0, pl.ds(start, TILE_ROWS), k * 128 : (k + 1) * 128] = cos * w
-                o_ref[0, pl.ds(start, TILE_ROWS), (k + 1) * 128 : (k + 2) * 128] = sin * (x * (w * w))
-
-            @pl.when(jnp.logical_not(any_entry))
-            def _():
-                o_ref[0, pl.ds(start, TILE_ROWS), k * 128 : (k + 2) * 128] = jnp.zeros((TILE_ROWS, 256), f32)
-
-        put(0, w_direct != 0, jnp.full((1, 128), w_direct, jnp.int32).astype(f32), freq_direct)
-        w = jnp.where(col == 0, w_extra, w_mirror).astype(f32)
-        put(2, jnp.logical_or(w_mirror != 0, w_extra != 0), w, freq_mirror)
+        other = DET - 1 - t
+        edge = jnp.where(t == 0, DET // 2, DET - t)
+        i = start + row
+        freq_y = i.astype(f32) * FREQ_STEP
+        freq_n = jnp.where(i == 0, -HALF * FREQ_STEP, -freq_y)
+
+        def load(k, t):
+            return flags_ref[k * BPD * DET + b * DET + t]
+
+        def direct(t):
+            return load(0, t), jnp.full((1, 128), load(0, t), jnp.int32).astype(f32)
+
+        def mirror(t):
+            w, w_extra = load(1, t), load(2, t)
+            return jnp.abs(w) + jnp.abs(w_extra), jnp.where(col == 0, w_extra, w).astype(f32)
+
+        for k, weights, freq_x in ((0, direct, freq_direct), (2, mirror, freq_mirror)):
+            any_here, w_here = weights(t)
+            put(k, start, any_here != 0, w_here, freq_x, freq_y)
+            any_other, w_other = weights(other)
+            any_edge, w_edge = weights(edge)
+            w = jnp.where(row == 0, w_edge, w_other)
+            put(k + 4, start, jnp.abs(any_other) + jnp.abs(any_edge) != 0, w, freq_x, freq_n)
         return 0
 
-    lax.fori_loop(0, DET, tile, 0)
+    lax.fori_loop(0, HALF // TILE_ROWS, tile, 0)
 
 
 def column_kernel(meta_ref, r_ref, phase_hbm, pick_hbm, table_ref, o_ref, *scratch):
@@ -183,57 +220,84 @@
     lane = lax.broadcasted_iota(jnp.int32, (1, 128), 1)
     special = meta_ref[1] * COLS + lane % COLS == 0
     keep = jnp.where(special, 0.0, 1.0)
-    size = GROUP * 256
-    step = 32
-
-    def products(g):
-        pq_ref[g % 2] = jnp.dot(table_ref[...], r_ref[:, g * size : (g + 1) * size], preferred_element_type=f32)
+
+    def products(b):
+        left = table_ref[HALF : 2 * HALF + LEFT]
+        right = r_ref[:, b * 256 : (b + 1) * 256]
+        lanes = slice(b % GROUP * 256, b % GROUP * 256 + 256)
+        pq_ref[0, :, lanes] = jnp.dot(left, right, preferred_element_type=f32)
 
     def lunes(g):
-        for i in range(GROUP):
-            copies[g * GROUP + i].wait()
-        for q in range(0, N, step):
-            sums = [0.0] * 4 if g == 0 else [acc_ref[q : q + step, k * 128 : (k + 1) * 128] for k in range(4)]
+        for q in range(0, HALF, STEP):
+            here = slice(q, q + STEP)
+            if g == 0:
+                sums = [0.0] * 8
+            else:
+                sums = [acc_ref[here, k * 128 : (k + 1) * 128] for k in range(8)]
             for i in range(GROUP):
-                here = slice(i * 256, i * 256 + 128)
-                there = slice(i * 256 + 128, i * 256 + 256)
-                p1 = pq_ref[g % 2, q : q + step, here]
-                p3 = pq_ref[g % 2, q : q + step, there]
-                p2 = pq_ref[g % 2, N + q : N + q + step, here]
-                p4 = pq_ref[g % 2, N + q : N + q + step, there]
-                cos, sin, cos_m, sin_m = [
-                    phase_ref[g * GROUP + i, q : q + step, k * 128 : (k + 1) * 128] for k in range(4)
-                ]
-                g_re = p1 + keep * p4
-                g_im = keep * p3 - p2
-                m_re = jnp.where(special, p3, p1 - p4)
-                m_im = jnp.where(special, p4, p3 + p2)
-                sums[0] += g_re * cos - g_im * sin
-                sums[1] += m_re * cos_m + m_im * sin_m
-                sums[2] += g_re * sin + g_im * cos
-                sums[3] += m_re * sin_m - m_im * cos_m
-            for k in range(4):
-                acc_ref[q : q + step, k * 128 : (k + 1) * 128] = sums[k]
-
-    products(0)
-    for g in range(1, BPD // GROUP):
-        products(g)
-        lunes(g - 1)
-    lunes(BPD // GROUP - 1)
-
-    copies[BPD].wait()
-    lune = jnp.dot(acc_ref[...].astype(bf16), pick_ref[...], preferred_element_type=f32)
-    high = lune.astype(bf16).astype(f32)
-    is_high = lax.broadcasted_iota(jnp.int32, (N, 256), 1) % 128 < 64
-    packed = jnp.where(is_high, high, lune - high).astype(bf16)
-    out_ref[...] = jnp.dot(table_ref[:N], packed[:, :128], preferred_element_type=f32) + jnp.dot(
-        table_ref[N:], packed[:, 128:], preferred_element_type=f32
-    )
+                re = slice(i * 256, i * 256 + 128)
+                im = slice(i * 256 + 128, i * 256 + 256)
+                p1 = pq_ref[0, HALF + q : HALF + q + STEP, re]
+                p3 = pq_ref[0, HALF + q : HALF + q + STEP, im]
+                p2 = pq_ref[0, here, re]
+                p4 = pq_ref[0, here, im]
+                phase = [phase_ref[g * GROUP + i, here, k * 128 : (k + 1) * 128].astype(f32) for k in range(8)]
+                k3 = keep * p3
+                k4 = keep * p4
+                n1, n3, nk3 = p1, p3, k3
+                if q == 0:
+                    first = lax.broadcasted_iota(jnp.int32, (STEP, 128), 0) == 0
+                    n1 = jnp.where(first, pq_ref[0, 2 * HALF : 2 * HALF + 1, re], p1)
+                    n3 = jnp.where(first, pq_ref[0, 2 * HALF : 2 * HALF + 1, im], p3)
+                    nk3 = keep * n3
+                pairs = (
+                    (p1 + k4, k3 - p2),
+                    (jnp.where(special, p3, p1 - k4), -jnp.where(special, p4, k3 + p2)),
+                    (n1 - k4, nk3 + p2),
+                    (jnp.where(special, n3, n1 + k4), jnp.where(special, p4, p2 - nk3)),
+                )
+                for j, (g_re, g_im) in enumerate(pairs):
+                    cos, sin = phase[2 * j], phase[2 * j + 1]
+                    k = (j // 2) * 4 + j % 2
+                    sums[k] += g_re * cos - g_im * sin
+                    sums[k + 2] += g_re * sin + g_im * cos
+            for k in range(8):
+                acc_ref[here, k * 128 : (k + 1) * 128] = sums[k]
+
+    for b in range(GROUP):
+        products(b)
+    for copy in copies[:GROUP]:
+        copy.wait()
+    for g in range(BPD // GROUP):
+        for copy in copies[(g + 1) * GROUP : (g + 2) * GROUP]:
+            copy.wait()
+        lunes(g)
+        if g + 1 < BPD // GROUP:
+            for i in range(GROUP):
+                products((g + 1) * GROUP + i)
+
+    plain = acc_ref[:, :N]
+    negated = acc_ref[:, N:]
+    inner = jnp.where(lax.broadcasted_iota(jnp.int32, (HALF, N), 0) == 0, 0.0, negated)
+    even_part = jnp.concatenate([plain + inner, negated[:8]], axis=0).astype(bf16)
+    odd_part = (plain - inner).astype(bf16)
+    even_part = jnp.dot(even_part, pick_ref[:, :128], preferred_element_type=f32)
+    odd_part = jnp.dot(odd_part, pick_ref[:, 128:], preferred_element_type=f32)
+    nyquist = even_part[HALF : HALF + 1]
+    first = lane < 64
+
+    def split(v):
+        high = v.astype(bf16).astype(f32)
+        return jnp.where(first, high, v - high).astype(bf16)
+
+    by_sin = jnp.dot(table_ref[:N, :HALF], split(odd_part), preferred_element_type=f32)
+    by_cos = jnp.dot(table_ref[N:, :HALF], split(even_part[:HALF]), preferred_element_type=f32)
+    out_ref[:HALF] = by_cos[:HALF] + by_sin[HALF:]
+    out_ref[HALF:] = by_cos[HALF:] + by_sin[:HALF]
     even = out_ref[pl.ds(0, N // 2, stride=2), :]
     odd = out_ref[pl.ds(1, N // 2, stride=2), :]
-    first = lane < 64
     out = jnp.where(first, even, odd) + pltpu.roll(jnp.where(first, odd, even), 64, 1)
-    o_ref[...] = out.astype(bf16)
+    o_ref[...] = (out + jnp.where(first, nyquist, -nyquist)).astype(bf16)
 
 
 def last_kernel(y_ref, table_ref, o_ref):
@@ -307,9 +371,10 @@
         scratch_shapes=[
             pltpu.VMEM((BPD * BLK, ROWS, N), bf16),
             pltpu.VMEM((N, N), bf16),
+            pltpu.VMEM((BLK * ROWS, N), f32),
             pltpu.VMEM((SCAN, ROWS, BPD * 256), bf16),
             pltpu.SemaphoreType.DMA((BPD + 1,)),
-            pltpu.SemaphoreType.DMA((BPD,)),
+            pltpu.SemaphoreType.DMA((len(SENDS),)),
         ],
         compiler_params=pltpu.CompilerParams(vmem_limit_bytes=10 << 20),
         name="rows",
@@ -321,8 +386,8 @@
         phase_kernel,
         grid=(BPD,),
         in_specs=[smem, smem, smem],
-        out_specs=[pl.BlockSpec((1, N, N), lambda b: (b, 0, 0)), pl.BlockSpec((N, 256), lambda b: (0, 0))],
-        out_shape=[pltpu.HBM((BPD, N, N), f32), pltpu.HBM((N, 256), bf16)],
+        out_specs=[pl.BlockSpec((1, HALF, 2 * N), lambda b: (b, 0, 0)), pl.BlockSpec((N, 256), lambda b: (0, 0))],
+        out_shape=[pltpu.HBM((BPD, HALF, 2 * N), bf16), pltpu.HBM((N, 256), bf16)],
         compiler_params=pltpu.CompilerParams(vmem_limit_bytes=8 << 20),
         name="phases",
     )(meta, flags, aberrations)
@@ -333,10 +398,10 @@
         out_specs=vmem,
         out_shape=jax.ShapeDtypeStruct((N // 2, 128), bf16),
         scratch_shapes=[
-            pltpu.VMEM((2, 2 * N, GROUP * 256), f32),
-            pltpu.VMEM((N, N), f32),
+            pltpu.VMEM((1, HALF + LEFT, GROUP * 256), f32),
+            pltpu.VMEM((HALF, 2 * N), f32),
             pltpu.VMEM((N, 128), f32),
-            pltpu.VMEM((BPD, N, N), f32),
+            pltpu.VMEM((BPD, HALF, 2 * N), bf16),
             pltpu.VMEM((N, 256), bf16),
             pltpu.SemaphoreType.DMA((BPD + 1,)),
         ],

time: 71.9 us -> 69.5 us (0.967)
  Pallas kernels: 22.3 us -> 19.2 us
    pallas_call x1, Pallas kernels: 6.01 us -> 4.02 us  [shards(): pl.pallas_call(row_kernel, in_specs=[hbm, hbm], out_specs=hbm, out_shape=...]
  transfers between devices with their start and end apart: 1 -> 1, of which waited for: 1 -> 1; matrix products, arithmetic and copies ran while one was open for 6% -> 6% of each run, Pallas kernels for 13% -> 12%
where the time goes in v3:
time: 69.5 us; the launch traced here: 69.2 us
  waiting for transfers between devices  19.4 us (28%)
  Pallas kernels  19.2 us (28%)
  blocking collectives  18.7 us (27%)
  starting transfers between devices  7.72 us (11%)
  local copies, waits for them, and re-layouts  2.49 us (4%)
  other arithmetic  1.59 us (2%)
    all_to_all x1, waiting for transfers between devices, shards(): lax.all_to_all(rows.reshape(N, BPD * 256), 'scan', 0, 0, tiled=True)  19.4 us
    all_to_all x1, blocking collectives, shards(): lax.all_to_all(back.reshape(DET * SCAN, 2, 128), ('det', 'scan'), 0, 0, t...  18.7 us
    pallas_call x1, Pallas kernels, shards(): pl.pallas_call(phase_kernel, grid=(BPD,), in_specs=[smem, smem, smem], ou...  8.3 us
    all_to_all x1, starting transfers between devices, shards(): lax.all_to_all(rows.reshape(N, BPD * 256), 'scan', 0, 0, tiled=True)  7.72 us
    pallas_call x1, Pallas kernels, shards(): pl.pallas_call(column_kernel, in_specs=[smem, vmem, hbm, hbm, vmem], out_...  5.9 us
    pallas_call x1, Pallas kernels, shards(): pl.pallas_call(row_kernel, in_specs=[hbm, hbm], out_specs=hbm, out_shape=...  4.02 us
  transfers between devices with their start and end apart: 1, of which 1 were waited for; matrix products, arithmetic and copies ran while one was open for 6% of the time, Pallas kernels for 12%

profile of v3, /device:TPU:1, one launch (start us, length us, event | category | flops | bytes accessed | tf_op | source)
XLA Modules:
  0.0 69.2 jit_solution(2491320923842307652)
XLA Ops:
  0.0 0.0 copy-start
  0.0 4.0 %rows.1 = bf16[16,32,2304]{2,1,0:T(8,128)(2,1)} custom-call(bf16[72,32,512]{2,1,0:T(8,128)(2,1)} %x_hbm.1, bf16[512,512]{1,0:T(8,128)(2,1)} %constant.58.clone.table_hbm), custom_call_target="tpu_custom_call" | custom-call | tf_op jit(solution)/shard_map/rows/pallas_call | solution.py:366
  4.0 0.0 copy-start.4
  4.0 0.0 copy-start.3
  4.1 0.0 copy-start.1
  4.1 7.7 %all-to-all-start = ((bf16[16,32,2304]{2,1,0:T(8,128)(2,1)}), bf16[16,32,2304]{2,1,0:T(8,128)(2,1)S(1)}, u32[]{:S(2)}, u32[]{:S(2)}) async-start(bf16[16,32,2304]{2,1,0:T(8,128)(2,1)} %rows.1), calls=%async_computation | async-start | bytes 4718592 | tf_op jit(solution)/shard_map/all_to_all | solution.py:383
  11.8 0.1 compare_and_fusion
  11.9 0.0 copy-done
  11.9 1.2 %gather_fusion.1 = s32[3,8,16]{2,0,1:T(4,128)} fusion(s32[8,16,16]{2,1,0:T(8,128)S(1)} %copy-done, s32[1024]{0:T(1024)S(1)} %pad_clamp_fusion), kind=kCustom, calls=%fused_computation.1.clone | custom fusion | bytes 3084 | tf_op jit(solution)/shard_map/jit(_take)/gather | solution.py:349
  13.1 0.0 copy-done.4
  13.1 1.2 %gather_fusion = s32[3,8,16]{2,0,1:T(4,128)} fusion(s32[8,16,16]{2,1,0:T(8,128)S(1)} %copy-done.4, s32[1024]{0:T(1024)S(1)} %pad_clamp_fusion), kind=kCustom, calls=%fused_computation.clone | custom fusion | bytes 3084 | tf_op jit(solution)/shard_map/jit(_take)/gather | solution.py:348
  14.3 0.8 %select_bitcast_fusion.1 = (s32[8,3,16]{2,1,0:T(4,128)S(1)}, s32[8,3,16]{2,1,0:T(4,128)S(1)}) fusion(s32[3,8,16]{2,0,1:T(4,128)} %gather_fusion, pred[3]{0:T(512)(128)(4,1)S(1)} %get-tuple-element.10, s32[3,8,16]{2,0,1:T(4,128)} %gather_fusion.1), kind=kLoop, calls=%fused_computation.4 | loop fusion | flops 768 | bytes 6147 | tf_op jit(solution)/shard_map/jit(_take)/select_n | solution.py:348
  15.1 0.6 select_reduce_fusion
  15.7 0.1 reshape.24.flags_ref
  15.8 0.1 pad_add_fusion.meta_ref
  15.9 0.0 copy-done.3
  15.9 8.3 %phases.1 = (bf16[9,256,1024]{2,1,0:T(8,128)(2,1)}, bf16[512,256]{1,0:T(8,128)(2,1)}) custom-call(s32[2]{0:T(128)S(1)} %pad_add_fusion.meta_ref, s32[216]{0:T(256)S(1)} %reshape.24.flags_ref, f32[3]{0:T(128)S(1)} %copy-done.3), custom_call_target="tpu_custom_call" | custom-call | tf_op jit(solution)/shard_map/phases/pallas_call | solution.py:385
  24.2 19.4 %all-to-all-done = bf16[16,32,2304]{2,1,0:T(8,128)(2,1)S(1)} async-done(((bf16[16,32,2304]{2,1,0:T(8,128)(2,1)}), bf16[16,32,2304]{2,1,0:T(8,128)(2,1)S(1)}, u32[]{:S(2)}, u32[]{:S(2)}) %all-to-all-start) | async-done | bytes 2359328 | tf_op jit(solution)/shard_map/all_to_all | solution.py:383
  43.6 0.0 copy-done.1
  43.6 0.0 copy-start.2
  43.6 5.9 %columns.1 = bf16[256,128]{1,0:T(8,128)(2,1)S(1)} custom-call(s32[2]{0:T(128)S(1)} %pad_add_fusion.meta_ref, bf16[512,2304]{1,0:T(8,128)(2,1)S(1)} %bitcast.13, bf16[9,256,1024]{2,1,0:T(8,128)(2,1)} %get-tuple-element.8.phase_hbm, bf16[512,256]{1,0:T(8,128)(2,1)} %get-tuple-element.9.pick_hbm, bf16[1024,512]{1,0:T(8,128)(2,1)S(1)} %copy-done.1), custom_call_target="tpu_custom_call" | custom-call | tf_op jit(solution)/shard_map/columns/pallas_call | solution.py:395
  49.5 18.7 %all_to_all.13 = bf16[128,2,128]{2,1,0:T(2,128)(2,1)S(1)} all-to-all(bf16[128,2,128]{2,1,0:T(2,128)(2,1)S(1)} %bitcast.14), channel_id=1, replica_groups=mesh['det'=8,'scan'=16] {'det','scan'}, dimensions={0} | all-to-all | bytes 131072 | tf_op jit(solution)/shard_map/all_to_all | solution.py:412
  68.2 0.0 copy-done.2
  68.2 1.0 %last.1 = f32[2,4,512]{2,1,0:T(4,128)} custom-call(bf16[256,128]{1,0:T(8,128)(2,1)S(1)} %bitcast.15, bf16[512,1024]{1,0:T(8,128)(2,1)S(1)} %copy-done.2), custom_call_target="tpu_custom_call" | custom-call | tf_op jit(solution)/shard_map/last/pallas_call | solution.py:414
  (4 shorter events, 0.0 us)
Async XLA Ops:
  0.0 11.9 %copy-start = (s32[8,16,16]{2,1,0:T(8,128)S(1)}, s32[8,16,16]{2,1,0:T(8,128)}, u32[]{:S(2)}) copy-start(s32[8,16,16]{2,1,0:T(8,128)} %param.12) | copy-start | bytes 24580
  4.0 9.1 %copy-start.4 = (s32[8,16,16]{2,1,0:T(8,128)S(1)}, s32[8,16,16]{2,1,0:T(8,128)}, u32[]{:S(2)}) copy-start(s32[8,16,16]{2,1,0:T(8,128)} %param.11) | copy-start | bytes 24580
  4.0 11.9 %copy-start.3 = (f32[3]{0:T(128)S(1)}, f32[3]{0:T(128)}, u32[]{:S(2)}) copy-start(f32[3]{0:T(128)} %ab_ref.1) | copy-start | bytes 40
  4.1 39.6 %copy-start.1 = (bf16[1024,512]{1,0:T(8,128)(2,1)S(1)}, bf16[1024,512]{1,0:T(8,128)(2,1)}, u32[]{:S(2)}) copy-start(bf16[1024,512]{1,0:T(8,128)(2,1)} %constant.59.clone.table_ref) | copy-start | bytes 3145732
  4.1 39.6 %all-to-all-start = ((bf16[16,32,2304]{2,1,0:T(8,128)(2,1)}), bf16[16,32,2304]{2,1,0:T(8,128)(2,1)S(1)}, u32[]{:S(2)}, u32[]{:S(2)}) async-start(bf16[16,32,2304]{2,1,0:T(8,128)(2,1)} %rows.1), calls=%async_computation | async-start | bytes 4718592 | tf_op jit(solution)/shard_map/all_to_all | solution.py:383
  43.6 24.6 %copy-start.2 = (bf16[512,1024]{1,0:T(8,128)(2,1)S(1)}, bf16[512,1024]{1,0:T(8,128)(2,1)}, u32[]{:S(2)}) copy-start(bf16[512,1024]{1,0:T(8,128)(2,1)} %constant.60.clone.table_ref) | copy-start | bytes 3145732

commit v4 on v3

--- a/solution.py
+++ b/solution.py
@@ -16,11 +16,10 @@
 BPD = 9
 HALF = N // 2
 LEFT = HALF + 8
-GROUP = 3
+GROUPS = (2, 2, 3, 2)
 STEP = 16
 WAITS = {0: (1, 2), 2: (3, 4, 5, 6, 7, 8)}
 SENDS = (2, 5, 7, 8)
-PIECE = 64
 COLS = 16
 ROWS = N // SCAN
 TILE_ROWS = N // DET
@@ -210,7 +209,7 @@
 
 
 def column_kernel(meta_ref, r_ref, phase_hbm, pick_hbm, table_ref, o_ref, *scratch):
-    pq_ref, acc_ref, out_ref, phase_ref, pick_ref, sems = scratch
+    pq_refs, acc_ref, even_ref, odd_ref, out_ref, phase_ref, pick_ref, sems = scratch[:2], *scratch[2:]
     f32 = jnp.float32
     bf16 = jnp.bfloat16
     copies = [pltpu.make_async_copy(phase_hbm.at[b], phase_ref.at[b], sems.at[b]) for b in range(BPD)]
@@ -220,35 +219,39 @@
     lane = lax.broadcasted_iota(jnp.int32, (1, 128), 1)
     special = meta_ref[1] * COLS + lane % COLS == 0
     keep = jnp.where(special, 0.0, 1.0)
-
-    def products(b):
+    starts = [sum(GROUPS[:g]) for g in range(len(GROUPS))]
+
+    def products(g):
         left = table_ref[HALF : 2 * HALF + LEFT]
-        right = r_ref[:, b * 256 : (b + 1) * 256]
-        lanes = slice(b % GROUP * 256, b % GROUP * 256 + 256)
-        pq_ref[0, :, lanes] = jnp.dot(left, right, preferred_element_type=f32)
+        pq_ref = pq_refs[g > 0]
+        for i in range(GROUPS[g]):
+            b = starts[g] + i
+            right = r_ref[:, b * 256 : (b + 1) * 256]
+            pq_ref[:, i * 256 : (i + 1) * 256] = jnp.dot(left, right, preferred_element_type=f32)
 
     def lunes(g):
+        pq_ref = pq_refs[g > 0]
         for q in range(0, HALF, STEP):
             here = slice(q, q + STEP)
+            first = lax.broadcasted_iota(jnp.int32, (STEP, 128), 0) == 0
             if g == 0:
                 sums = [0.0] * 8
             else:
                 sums = [acc_ref[here, k * 128 : (k + 1) * 128] for k in range(8)]
-            for i in range(GROUP):
+            for i in range(GROUPS[g]):
                 re = slice(i * 256, i * 256 + 128)
                 im = slice(i * 256 + 128, i * 256 + 256)
-                p1 = pq_ref[0, HALF + q : HALF + q + STEP, re]
-                p3 = pq_ref[0, HALF + q : HALF + q + STEP, im]
-                p2 = pq_ref[0, here, re]
-                p4 = pq_ref[0, here, im]
-                phase = [phase_ref[g * GROUP + i, here, k * 128 : (k + 1) * 128].astype(f32) for k in range(8)]
+                p1 = pq_ref[HALF + q : HALF + q + STEP, re]
+                p3 = pq_ref[HALF + q : HALF + q + STEP, im]
+                p2 = pq_ref[here, re]
+                p4 = pq_ref[here, im]
+                phase = [phase_ref[starts[g] + i, here, k * 128 : (k + 1) * 128].astype(f32) for k in range(8)]
                 k3 = keep * p3
                 k4 = keep * p4
                 n1, n3, nk3 = p1, p3, k3
                 if q == 0:
-                    first = lax.broadcasted_iota(jnp.int32, (STEP, 128), 0) == 0
-                    n1 = jnp.where(first, pq_ref[0, 2 * HALF : 2 * HALF + 1, re], p1)
-                    n3 = jnp.where(first, pq_ref[0, 2 * HALF : 2 * HALF + 1, im], p3)
+                    n1 = jnp.where(first, pq_ref[2 * HALF : 2 * HALF + 1, re], p1)
+                    n3 = jnp.where(first, pq_ref[2 * HALF : 2 * HALF + 1, im], p3)
                     nk3 = keep * n3
                 pairs = (
                     (p1 + k4, k3 - p2),
@@ -261,34 +264,38 @@
                     k = (j // 2) * 4 + j % 2
                     sums[k] += g_re * cos - g_im * sin
                     sums[k + 2] += g_re * sin + g_im * cos
-            for k in range(8):
-                acc_ref[here, k * 128 : (k + 1) * 128] = sums[k]
-
-    for b in range(GROUP):
-        products(b)
-    for copy in copies[:GROUP]:
-        copy.wait()
-    for g in range(BPD // GROUP):
-        for copy in copies[(g + 1) * GROUP : (g + 2) * GROUP]:
-            copy.wait()
+            for k in range(4):
+                lanes = slice(k * 128, (k + 1) * 128)
+                if g + 1 < len(GROUPS):
+                    acc_ref[here, lanes] = sums[k]
+                    acc_ref[here, N + k * 128 : N + (k + 1) * 128] = sums[k + 4]
+                    continue
+                negated = sums[k + 4]
+                if q == 0:
+                    even_ref[HALF : HALF + STEP, lanes] = negated.astype(bf16)
+                    negated = jnp.where(first, 0.0, negated)
+                even_ref[here, lanes] = (sums[k] + negated).astype(bf16)
+                odd_ref[here, lanes] = (sums[k] - negated).astype(bf16)
+
+    products(0)
+    products(1)
+    for g in range(len(GROUPS)):
+        for b in range(starts[g], starts[g] + GROUPS[g]):
+            copies[b].wait()
+        if g + 1 == len(GROUPS):
+            copies[BPD].wait()
         lunes(g)
-        if g + 1 < BPD // GROUP:
-            for i in range(GROUP):
-                products((g + 1) * GROUP + i)
-
-    plain = acc_ref[:, :N]
-    negated = acc_ref[:, N:]
-    inner = jnp.where(lax.broadcasted_iota(jnp.int32, (HALF, N), 0) == 0, 0.0, negated)
-    even_part = jnp.concatenate([plain + inner, negated[:8]], axis=0).astype(bf16)
-    odd_part = (plain - inner).astype(bf16)
-    even_part = jnp.dot(even_part, pick_ref[:, :128], preferred_element_type=f32)
-    odd_part = jnp.dot(odd_part, pick_ref[:, 128:], preferred_element_type=f32)
+        if 0 < g < len(GROUPS) - 1:
+            products(g + 1)
+
+    even_part = jnp.dot(even_ref[...], pick_ref[:, :128], preferred_element_type=f32)
+    odd_part = jnp.dot(odd_ref[...], pick_ref[:, 128:], preferred_element_type=f32)
     nyquist = even_part[HALF : HALF + 1]
-    first = lane < 64
+    left_half = lane < 64
 
     def split(v):
         high = v.astype(bf16).astype(f32)
-        return jnp.where(first, high, v - high).astype(bf16)
+        return jnp.where(left_half, high, v - high).astype(bf16)
 
     by_sin = jnp.dot(table_ref[:N, :HALF], split(odd_part), preferred_element_type=f32)
     by_cos = jnp.dot(table_ref[N:, :HALF], split(even_part[:HALF]), preferred_element_type=f32)
@@ -296,8 +303,8 @@
     out_ref[HALF:] = by_cos[HALF:] + by_sin[:HALF]
     even = out_ref[pl.ds(0, N // 2, stride=2), :]
     odd = out_ref[pl.ds(1, N // 2, stride=2), :]
-    out = jnp.where(first, even, odd) + pltpu.roll(jnp.where(first, odd, even), 64, 1)
-    o_ref[...] = (out + jnp.where(first, nyquist, -nyquist)).astype(bf16)
+    out = jnp.where(left_half, even, odd) + pltpu.roll(jnp.where(left_half, odd, even), 64, 1)
+    o_ref[...] = (out + jnp.where(left_half, nyquist, -nyquist)).astype(bf16)
 
 
 def last_kernel(y_ref, table_ref, o_ref):
@@ -398,8 +405,11 @@
         out_specs=vmem,
         out_shape=jax.ShapeDtypeStruct((N // 2, 128), bf16),
         scratch_shapes=[
-            pltpu.VMEM((1, HALF + LEFT, GROUP * 256), f32),
+            pltpu.VMEM((HALF + LEFT, GROUPS[0] * 256), f32),
+            pltpu.VMEM((HALF + LEFT, max(GROUPS) * 256), f32),
             pltpu.VMEM((HALF, 2 * N), f32),
+            pltpu.VMEM((HALF + STEP, N), bf16),
+            pltpu.VMEM((HALF, N), bf16),
             pltpu.VMEM((N, 128), f32),
             pltpu.VMEM((BPD, HALF, 2 * N), bf16),
             pltpu.VMEM((N, 256), bf16),

time: 69.5 us -> 68.9 us (level)
  no operation moved by 1% of the time
where the time goes in v4:
time: 68.9 us; the launch traced here: 68.6 us
  waiting for transfers between devices  19.3 us (28%)
  Pallas kernels  18.7 us (27%)
  blocking collectives  18.7 us (27%)
  starting transfers between devices  7.72 us (11%)
  local copies, waits for them, and re-layouts  2.49 us (4%)
  other arithmetic  1.59 us (2%)
    all_to_all x1, waiting for transfers between devices, shards(): lax.all_to_all(rows.reshape(N, BPD * 256), 'scan', 0, 0, tiled=True)  19.3 us
    all_to_all x1, blocking collectives, shards(): lax.all_to_all(back.reshape(DET * SCAN, 2, 128), ('det', 'scan'), 0, 0, t...  18.7 us
    pallas_call x1, Pallas kernels, shards(): pl.pallas_call(phase_kernel, grid=(BPD,), in_specs=[smem, smem, smem], ou...  8.38 us
    all_to_all x1, starting transfers between devices, shards(): lax.all_to_all(rows.reshape(N, BPD * 256), 'scan', 0, 0, tiled=True)  7.72 us
    pallas_call x1, Pallas kernels, shards(): pl.pallas_call(column_kernel, in_specs=[smem, vmem, hbm, hbm, vmem], out_...  5.29 us
    pallas_call x1, Pallas kernels, shards(): pl.pallas_call(row_kernel, in_specs=[hbm, hbm], out_specs=hbm, out_shape=...  4.02 us
  transfers between devices with their start and end apart: 1, of which 1 were waited for; matrix products, arithmetic and copies ran while one was open for 6% of the time, Pallas kernels for 12%

profile of v4, /device:TPU:1, one launch (start us, length us, event | category | flops | bytes accessed | tf_op | source)
XLA Modules:
  0.0 68.6 jit_solution(3214518202439144468)
XLA Ops:
  0.0 0.0 copy-start
  0.0 4.0 %rows.1 = bf16[16,32,2304]{2,1,0:T(8,128)(2,1)} custom-call(bf16[72,32,512]{2,1,0:T(8,128)(2,1)} %x_hbm.1, bf16[512,512]{1,0:T(8,128)(2,1)} %constant.58.clone.table_hbm), custom_call_target="tpu_custom_call" | custom-call | tf_op jit(solution)/shard_map/rows/pallas_call | solution.py:373
  4.0 0.0 copy-start.4
  4.0 0.0 copy-start.3
  4.1 0.0 copy-start.1
  4.1 7.7 %all-to-all-start = ((bf16[16,32,2304]{2,1,0:T(8,128)(2,1)}), bf16[16,32,2304]{2,1,0:T(8,128)(2,1)S(1)}, u32[]{:S(2)}, u32[]{:S(2)}) async-start(bf16[16,32,2304]{2,1,0:T(8,128)(2,1)} %rows.1), calls=%async_computation | async-start | bytes 4718592 | tf_op jit(solution)/shard_map/all_to_all | solution.py:390
  11.8 0.1 compare_and_fusion
  11.9 0.0 copy-done
  11.9 1.2 %gather_fusion.1 = s32[3,8,16]{2,0,1:T(4,128)} fusion(s32[8,16,16]{2,1,0:T(8,128)S(1)} %copy-done, s32[1024]{0:T(1024)S(1)} %pad_clamp_fusion), kind=kCustom, calls=%fused_computation.1.clone | custom fusion | bytes 3084 | tf_op jit(solution)/shard_map/jit(_take)/gather | solution.py:356
  13.1 0.0 copy-done.4
  13.1 1.2 %gather_fusion = s32[3,8,16]{2,0,1:T(4,128)} fusion(s32[8,16,16]{2,1,0:T(8,128)S(1)} %copy-done.4, s32[1024]{0:T(1024)S(1)} %pad_clamp_fusion), kind=kCustom, calls=%fused_computation.clone | custom fusion | bytes 3084 | tf_op jit(solution)/shard_map/jit(_take)/gather | solution.py:355
  14.3 0.8 %select_bitcast_fusion.1 = (s32[8,3,16]{2,1,0:T(4,128)S(1)}, s32[8,3,16]{2,1,0:T(4,128)S(1)}) fusion(s32[3,8,16]{2,0,1:T(4,128)} %gather_fusion, pred[3]{0:T(512)(128)(4,1)S(1)} %get-tuple-element.10, s32[3,8,16]{2,0,1:T(4,128)} %gather_fusion.1), kind=kLoop, calls=%fused_computation.4 | loop fusion | flops 768 | bytes 6147 | tf_op jit(solution)/shard_map/jit(_take)/select_n | solution.py:355
  15.1 0.6 select_reduce_fusion
  15.7 0.1 reshape.24.flags_ref
  15.8 0.1 pad_add_fusion.meta_ref
  15.9 0.0 copy-done.3
  15.9 8.4 %phases.1 = (bf16[9,256,1024]{2,1,0:T(8,128)(2,1)}, bf16[512,256]{1,0:T(8,128)(2,1)}) custom-call(s32[2]{0:T(128)S(1)} %pad_add_fusion.meta_ref, s32[216]{0:T(256)S(1)} %reshape.24.flags_ref, f32[3]{0:T(128)S(1)} %copy-done.3), custom_call_target="tpu_custom_call" | custom-call | tf_op jit(solution)/shard_map/phases/pallas_call | solution.py:392
  24.3 19.3 %all-to-all-done = bf16[16,32,2304]{2,1,0:T(8,128)(2,1)S(1)} async-done(((bf16[16,32,2304]{2,1,0:T(8,128)(2,1)}), bf16[16,32,2304]{2,1,0:T(8,128)(2,1)S(1)}, u32[]{:S(2)}, u32[]{:S(2)}) %all-to-all-start) | async-done | bytes 2359328 | tf_op jit(solution)/shard_map/all_to_all | solution.py:390
  43.6 0.0 copy-done.1
  43.6 0.0 copy-start.2
  43.6 5.3 %columns.1 = bf16[256,128]{1,0:T(8,128)(2,1)S(1)} custom-call(s32[2]{0:T(128)S(1)} %pad_add_fusion.meta_ref, bf16[512,2304]{1,0:T(8,128)(2,1)S(1)} %bitcast.13, bf16[9,256,1024]{2,1,0:T(8,128)(2,1)} %get-tuple-element.8.phase_hbm, bf16[512,256]{1,0:T(8,128)(2,1)} %get-tuple-element.9.pick_hbm, bf16[1024,512]{1,0:T(8,128)(2,1)S(1)} %copy-done.1), custom_call_target="tpu_custom_call" | custom-call | tf_op jit(solution)/shard_map/columns/pallas_call | solution.py:402
  48.9 18.7 %all_to_all.13 = bf16[128,2,128]{2,1,0:T(2,128)(2,1)S(1)} all-to-all(bf16[128,2,128]{2,1,0:T(2,128)(2,1)S(1)} %bitcast.14), channel_id=1, replica_groups=mesh['det'=8,'scan'=16] {'det','scan'}, dimensions={0} | all-to-all | bytes 131072 | tf_op jit(solution)/shard_map/all_to_all | solution.py:422
  67.6 0.0 copy-done.2
  67.6 1.0 %last.1 = f32[2,4,512]{2,1,0:T(4,128)} custom-call(bf16[256,128]{1,0:T(8,128)(2,1)S(1)} %bitcast.15, bf16[512,1024]{1,0:T(8,128)(2,1)S(1)} %copy-done.2), custom_call_target="tpu_custom_call" | custom-call | tf_op jit(solution)/shard_map/last/pallas_call | solution.py:424
  (4 shorter events, 0.0 us)
Async XLA Ops:
  0.0 11.9 %copy-start = (s32[8,16,16]{2,1,0:T(8,128)S(1)}, s32[8,16,16]{2,1,0:T(8,128)}, u32[]{:S(2)}) copy-start(s32[8,16,16]{2,1,0:T(8,128)} %param.12) | copy-start | bytes 24580
  4.0 9.1 %copy-start.4 = (s32[8,16,16]{2,1,0:T(8,128)S(1)}, s32[8,16,16]{2,1,0:T(8,128)}, u32[]{:S(2)}) copy-start(s32[8,16,16]{2,1,0:T(8,128)} %param.11) | copy-start | bytes 24580
  4.0 11.9 %copy-start.3 = (f32[3]{0:T(128)S(1)}, f32[3]{0:T(128)}, u32[]{:S(2)}) copy-start(f32[3]{0:T(128)} %ab_ref.1) | copy-start | bytes 40
  4.1 39.6 %copy-start.1 = (bf16[1024,512]{1,0:T(8,128)(2,1)S(1)}, bf16[1024,512]{1,0:T(8,128)(2,1)}, u32[]{:S(2)}) copy-start(bf16[1024,512]{1,0:T(8,128)(2,1)} %constant.59.clone.table_ref) | copy-start | bytes 3145732
  4.1 39.6 %all-to-all-start = ((bf16[16,32,2304]{2,1,0:T(8,128)(2,1)}), bf16[16,32,2304]{2,1,0:T(8,128)(2,1)S(1)}, u32[]{:S(2)}, u32[]{:S(2)}) async-start(bf16[16,32,2304]{2,1,0:T(8,128)(2,1)} %rows.1), calls=%async_computation | async-start | bytes 4718592 | tf_op jit(solution)/shard_map/all_to_all | solution.py:390
  43.6 24.0 %copy-start.2 = (bf16[512,1024]{1,0:T(8,128)(2,1)S(1)}, bf16[512,1024]{1,0:T(8,128)(2,1)}, u32[]{:S(2)}) copy-start(bf16[512,1024]{1,0:T(8,128)(2,1)} %constant.60.clone.table_ref) | copy-start | bytes 3145732

commit v5 on v4

--- a/solution.py
+++ b/solution.py
@@ -16,8 +16,8 @@
 BPD = 9
 HALF = N // 2
 LEFT = HALF + 8
-GROUPS = (2, 2, 3, 2)
-STEP = 16
+PIECE = 32
+STEP = 8
 WAITS = {0: (1, 2), 2: (3, 4, 5, 6, 7, 8)}
 SENDS = (2, 5, 7, 8)
 COLS = 16
@@ -209,43 +209,37 @@
 
 
 def column_kernel(meta_ref, r_ref, phase_hbm, pick_hbm, table_ref, o_ref, *scratch):
-    pq_refs, acc_ref, even_ref, odd_ref, out_ref, phase_ref, pick_ref, sems = scratch[:2], *scratch[2:]
+    pq_ref, even_ref, odd_ref, out_ref, phase_ref, pick_ref, sems = scratch
     f32 = jnp.float32
     bf16 = jnp.bfloat16
-    copies = [pltpu.make_async_copy(phase_hbm.at[b], phase_ref.at[b], sems.at[b]) for b in range(BPD)]
-    copies.append(pltpu.make_async_copy(pick_hbm, pick_ref, sems.at[BPD]))
+    copies = []
+    for i in range(HALF // PIECE):
+        piece = pl.ds(i * PIECE, PIECE)
+        copies.append(pltpu.make_async_copy(phase_hbm.at[:, piece], phase_ref.at[:, piece], sems.at[i]))
+    copies.append(pltpu.make_async_copy(pick_hbm, pick_ref, sems.at[HALF // PIECE]))
     for copy in copies:
         copy.start()
     lane = lax.broadcasted_iota(jnp.int32, (1, 128), 1)
     special = meta_ref[1] * COLS + lane % COLS == 0
     keep = jnp.where(special, 0.0, 1.0)
-    starts = [sum(GROUPS[:g]) for g in range(len(GROUPS))]
-
-    def products(g):
-        left = table_ref[HALF : 2 * HALF + LEFT]
-        pq_ref = pq_refs[g > 0]
-        for i in range(GROUPS[g]):
-            b = starts[g] + i
-            right = r_ref[:, b * 256 : (b + 1) * 256]
-            pq_ref[:, i * 256 : (i + 1) * 256] = jnp.dot(left, right, preferred_element_type=f32)
-
-    def lunes(g):
-        pq_ref = pq_refs[g > 0]
-        for q in range(0, HALF, STEP):
+    left = table_ref[HALF : 2 * HALF + LEFT]
+    for b in range(BPD):
+        lanes = slice(b * 256, (b + 1) * 256)
+        pq_ref[:, lanes] = jnp.dot(left, r_ref[:, lanes], preferred_element_type=f32)
+
+    def lunes(begin):
+        for q in range(begin, begin + PIECE, STEP):
             here = slice(q, q + STEP)
             first = lax.broadcasted_iota(jnp.int32, (STEP, 128), 0) == 0
-            if g == 0:
-                sums = [0.0] * 8
-            else:
-                sums = [acc_ref[here, k * 128 : (k + 1) * 128] for k in range(8)]
-            for i in range(GROUPS[g]):
+            sums = [0.0] * 8
+            for i in range(BPD):
                 re = slice(i * 256, i * 256 + 128)
                 im = slice(i * 256 + 128, i * 256 + 256)
                 p1 = pq_ref[HALF + q : HALF + q + STEP, re]
                 p3 = pq_ref[HALF + q : HALF + q + STEP, im]
                 p2 = pq_ref[here, re]
                 p4 = pq_ref[here, im]
-                phase = [phase_ref[starts[g] + i, here, k * 128 : (k + 1) * 128].astype(f32) for k in range(8)]
+                phase = [phase_ref[i, here, k * 128 : (k + 1) * 128].astype(f32) for k in range(8)]
                 k3 = keep * p3
                 k4 = keep * p4
                 n1, n3, nk3 = p1, p3, k3
@@ -266,10 +260,6 @@
                     sums[k + 2] += g_re * sin + g_im * cos
             for k in range(4):
                 lanes = slice(k * 128, (k + 1) * 128)
-                if g + 1 < len(GROUPS):
-                    acc_ref[here, lanes] = sums[k]
-                    acc_ref[here, N + k * 128 : N + (k + 1) * 128] = sums[k + 4]
-                    continue
                 negated = sums[k + 4]
                 if q == 0:
                     even_ref[HALF : HALF + STEP, lanes] = negated.astype(bf16)
@@ -277,17 +267,11 @@
                 even_ref[here, lanes] = (sums[k] + negated).astype(bf16)
                 odd_ref[here, lanes] = (sums[k] - negated).astype(bf16)
 
-    products(0)
-    products(1)
-    for g in range(len(GROUPS)):
-        for b in range(starts[g], starts[g] + GROUPS[g]):
-            copies[b].wait()
-        if g + 1 == len(GROUPS):
-            copies[BPD].wait()
-        lunes(g)
-        if 0 < g < len(GROUPS) - 1:
-            products(g + 1)
-
+    for i in range(HALF // PIECE):
+        copies[i].wait()
+        lunes(i * PIECE)
+
+    copies[-1].wait()
     even_part = jnp.dot(even_ref[...], pick_ref[:, :128], preferred_element_type=f32)
     odd_part = jnp.dot(odd_ref[...], pick_ref[:, 128:], preferred_element_type=f32)
     nyquist = even_part[HALF : HALF + 1]
@@ -405,15 +389,13 @@
         out_specs=vmem,
         out_shape=jax.ShapeDtypeStruct((N // 2, 128), bf16),
         scratch_shapes=[
-            pltpu.VMEM((HALF + LEFT, GROUPS[0] * 256), f32),
-            pltpu.VMEM((HALF + LEFT, max(GROUPS) * 256), f32),
-            pltpu.VMEM((HALF, 2 * N), f32),
+            pltpu.VMEM((HALF + LEFT, BPD * 256), f32),
             pltpu.VMEM((HALF + STEP, N), bf16),
             pltpu.VMEM((HALF, N), bf16),
             pltpu.VMEM((N, 128), f32),
             pltpu.VMEM((BPD, HALF, 2 * N), bf16),
             pltpu.VMEM((N, 256), bf16),
-            pltpu.SemaphoreType.DMA((BPD + 1,)),
+            pltpu.SemaphoreType.DMA((HALF // PIECE + 1,)),
         ],
         compiler_params=pltpu.CompilerParams(vmem_limit_bytes=36 << 20),
         name="columns",

time: 68.9 us -> 68.8 us (level)
  no operation moved by 1% of the time
where the time goes in v5:
time: 68.8 us; the launch traced here: 68.4 us
  waiting for transfers between devices  19.5 us (28%)
  blocking collectives  18.7 us (27%)
  Pallas kernels  18.4 us (27%)
  starting transfers between devices  7.72 us (11%)
  local copies, waits for them, and re-layouts  2.49 us (4%)
  other arithmetic  1.59 us (2%)
    all_to_all x1, waiting for transfers between devices, shards(): lax.all_to_all(rows.reshape(N, BPD * 256), 'scan', 0, 0, tiled=True)  19.5 us
    all_to_all x1, blocking collectives, shards(): lax.all_to_all(back.reshape(DET * SCAN, 2, 128), ('det', 'scan'), 0, 0, t...  18.7 us
    pallas_call x1, Pallas kernels, shards(): pl.pallas_call(phase_kernel, grid=(BPD,), in_specs=[smem, smem, smem], ou...  8.23 us
    all_to_all x1, starting transfers between devices, shards(): lax.all_to_all(rows.reshape(N, BPD * 256), 'scan', 0, 0, tiled=True)  7.72 us
    pallas_call x1, Pallas kernels, shards(): pl.pallas_call(column_kernel, in_specs=[smem, vmem, hbm, hbm, vmem], out_...  5.17 us
    pallas_call x1, Pallas kernels, shards(): pl.pallas_call(row_kernel, in_specs=[hbm, hbm], out_specs=hbm, out_shape=...  4.02 us
  transfers between devices with their start and end apart: 1, of which 1 were waited for; matrix products, arithmetic and copies ran while one was open for 6% of the time, Pallas kernels for 12%

profile of v5, /device:TPU:1, one launch (start us, length us, event | category | flops | bytes accessed | tf_op | source)
XLA Modules:
  0.0 68.4 jit_solution(10887962055686710059)
XLA Ops:
  0.0 0.0 copy-start
  0.0 4.0 %rows.1 = bf16[16,32,2304]{2,1,0:T(8,128)(2,1)} custom-call(bf16[72,32,512]{2,1,0:T(8,128)(2,1)} %x_hbm.1, bf16[512,512]{1,0:T(8,128)(2,1)} %constant.58.clone.table_hbm), custom_call_target="tpu_custom_call" | custom-call | tf_op jit(solution)/shard_map/rows/pallas_call | solution.py:357
  4.0 0.0 copy-start.4
  4.0 0.0 copy-start.3
  4.1 0.0 copy-start.1
  4.1 7.7 %all-to-all-start = ((bf16[16,32,2304]{2,1,0:T(8,128)(2,1)}), bf16[16,32,2304]{2,1,0:T(8,128)(2,1)S(1)}, u32[]{:S(2)}, u32[]{:S(2)}) async-start(bf16[16,32,2304]{2,1,0:T(8,128)(2,1)} %rows.1), calls=%async_computation | async-start | bytes 4718592 | tf_op jit(solution)/shard_map/all_to_all | solution.py:374
  11.8 0.1 compare_and_fusion
  11.9 0.0 copy-done
  11.9 1.2 %gather_fusion.1 = s32[3,8,16]{2,0,1:T(4,128)} fusion(s32[8,16,16]{2,1,0:T(8,128)S(1)} %copy-done, s32[1024]{0:T(1024)S(1)} %pad_clamp_fusion), kind=kCustom, calls=%fused_computation.1.clone | custom fusion | bytes 3084 | tf_op jit(solution)/shard_map/jit(_take)/gather | solution.py:340
  13.1 0.0 copy-done.4
  13.1 1.2 %gather_fusion = s32[3,8,16]{2,0,1:T(4,128)} fusion(s32[8,16,16]{2,1,0:T(8,128)S(1)} %copy-done.4, s32[1024]{0:T(1024)S(1)} %pad_clamp_fusion), kind=kCustom, calls=%fused_computation.clone | custom fusion | bytes 3084 | tf_op jit(solution)/shard_map/jit(_take)/gather | solution.py:339
  14.3 0.8 %select_bitcast_fusion.1 = (s32[8,3,16]{2,1,0:T(4,128)S(1)}, s32[8,3,16]{2,1,0:T(4,128)S(1)}) fusion(s32[3,8,16]{2,0,1:T(4,128)} %gather_fusion, pred[3]{0:T(512)(128)(4,1)S(1)} %get-tuple-element.10, s32[3,8,16]{2,0,1:T(4,128)} %gather_fusion.1), kind=kLoop, calls=%fused_computation.4 | loop fusion | flops 768 | bytes 6147 | tf_op jit(solution)/shard_map/jit(_take)/select_n | solution.py:339
  15.1 0.6 select_reduce_fusion
  15.7 0.1 reshape.24.flags_ref
  15.8 0.1 pad_add_fusion.meta_ref
  15.9 0.0 copy-done.3
  15.9 8.2 %phases.1 = (bf16[9,256,1024]{2,1,0:T(8,128)(2,1)}, bf16[512,256]{1,0:T(8,128)(2,1)}) custom-call(s32[2]{0:T(128)S(1)} %pad_add_fusion.meta_ref, s32[216]{0:T(256)S(1)} %reshape.24.flags_ref, f32[3]{0:T(128)S(1)} %copy-done.3), custom_call_target="tpu_custom_call" | custom-call | tf_op jit(solution)/shard_map/phases/pallas_call | solution.py:376
  24.2 19.5 %all-to-all-done = bf16[16,32,2304]{2,1,0:T(8,128)(2,1)S(1)} async-done(((bf16[16,32,2304]{2,1,0:T(8,128)(2,1)}), bf16[16,32,2304]{2,1,0:T(8,128)(2,1)S(1)}, u32[]{:S(2)}, u32[]{:S(2)}) %all-to-all-start) | async-done | bytes 2359328 | tf_op jit(solution)/shard_map/all_to_all | solution.py:374
  43.6 0.0 copy-done.1
  43.6 0.0 copy-start.2
  43.6 5.2 %columns.1 = bf16[256,128]{1,0:T(8,128)(2,1)S(1)} custom-call(s32[2]{0:T(128)S(1)} %pad_add_fusion.meta_ref, bf16[512,2304]{1,0:T(8,128)(2,1)S(1)} %bitcast.13, bf16[9,256,1024]{2,1,0:T(8,128)(2,1)} %get-tuple-element.8.phase_hbm, bf16[512,256]{1,0:T(8,128)(2,1)} %get-tuple-element.9.pick_hbm, bf16[1024,512]{1,0:T(8,128)(2,1)S(1)} %copy-done.1), custom_call_target="tpu_custom_call" | custom-call | tf_op jit(solution)/shard_map/columns/pallas_call | solution.py:386
  48.8 18.7 %all_to_all.13 = bf16[128,2,128]{2,1,0:T(2,128)(2,1)S(1)} all-to-all(bf16[128,2,128]{2,1,0:T(2,128)(2,1)S(1)} %bitcast.14), channel_id=1, replica_groups=mesh['det'=8,'scan'=16] {'det','scan'}, dimensions={0} | all-to-all | bytes 131072 | tf_op jit(solution)/shard_map/all_to_all | solution.py:404
  67.5 0.0 copy-done.2
  67.5 1.0 %last.1 = f32[2,4,512]{2,1,0:T(4,128)} custom-call(bf16[256,128]{1,0:T(8,128)(2,1)S(1)} %bitcast.15, bf16[512,1024]{1,0:T(8,128)(2,1)S(1)} %copy-done.2), custom_call_target="tpu_custom_call" | custom-call | tf_op jit(solution)/shard_map/last/pallas_call | solution.py:406
  (4 shorter events, 0.0 us)
Async XLA Ops:
  0.0 11.9 %copy-start = (s32[8,16,16]{2,1,0:T(8,128)S(1)}, s32[8,16,16]{2,1,0:T(8,128)}, u32[]{:S(2)}) copy-start(s32[8,16,16]{2,1,0:T(8,128)} %param.12) | copy-start | bytes 24580
  4.0 9.1 %copy-start.4 = (s32[8,16,16]{2,1,0:T(8,128)S(1)}, s32[8,16,16]{2,1,0:T(8,128)}, u32[]{:S(2)}) copy-start(s32[8,16,16]{2,1,0:T(8,128)} %param.11) | copy-start | bytes 24580
  4.0 11.9 %copy-start.3 = (f32[3]{0:T(128)S(1)}, f32[3]{0:T(128)}, u32[]{:S(2)}) copy-start(f32[3]{0:T(128)} %ab_ref.1) | copy-start | bytes 40
  4.1 39.6 %copy-start.1 = (bf16[1024,512]{1,0:T(8,128)(2,1)S(1)}, bf16[1024,512]{1,0:T(8,128)(2,1)}, u32[]{:S(2)}) copy-start(bf16[1024,512]{1,0:T(8,128)(2,1)} %constant.59.clone.table_ref) | copy-start | bytes 3145732
  4.1 39.6 %all-to-all-start = ((bf16[16,32,2304]{2,1,0:T(8,128)(2,1)}), bf16[16,32,2304]{2,1,0:T(8,128)(2,1)S(1)}, u32[]{:S(2)}, u32[]{:S(2)}) async-start(bf16[16,32,2304]{2,1,0:T(8,128)(2,1)} %rows.1), calls=%async_computation | async-start | bytes 4718592 | tf_op jit(solution)/shard_map/all_to_all | solution.py:374
  43.6 23.9 %copy-start.2 = (bf16[512,1024]{1,0:T(8,128)(2,1)S(1)}, bf16[512,1024]{1,0:T(8,128)(2,1)}, u32[]{:S(2)}) copy-start(bf16[512,1024]{1,0:T(8,128)(2,1)} %constant.60.clone.table_ref) | copy-start | bytes 3145732

commit v6 on v5

--- a/solution.py
+++ b/solution.py
@@ -231,7 +231,7 @@
         for q in range(begin, begin + PIECE, STEP):
             here = slice(q, q + STEP)
             first = lax.broadcasted_iota(jnp.int32, (STEP, 128), 0) == 0
-            sums = [0.0] * 8
+            sums = [None] * 8
             for i in range(BPD):
                 re = slice(i * 256, i * 256 + 128)
                 im = slice(i * 256 + 128, i * 256 + 256)
@@ -249,15 +249,19 @@
                     nk3 = keep * n3
                 pairs = (
                     (p1 + k4, k3 - p2),
-                    (jnp.where(special, p3, p1 - k4), -jnp.where(special, p4, k3 + p2)),
+                    (jnp.where(special, p3, p1 - k4), jnp.where(special, p4, k3 + p2)),
                     (n1 - k4, nk3 + p2),
                     (jnp.where(special, n3, n1 + k4), jnp.where(special, p4, p2 - nk3)),
                 )
                 for j, (g_re, g_im) in enumerate(pairs):
                     cos, sin = phase[2 * j], phase[2 * j + 1]
                     k = (j // 2) * 4 + j % 2
-                    sums[k] += g_re * cos - g_im * sin
-                    sums[k + 2] += g_re * sin + g_im * cos
+                    if j == 1:
+                        terms = (g_re * cos + g_im * sin, g_re * sin - g_im * cos)
+                    else:
+                        terms = (g_re * cos - g_im * sin, g_re * sin + g_im * cos)
+                    for slot, term in zip((k, k + 2), terms):
+                        sums[slot] = term if sums[slot] is None else sums[slot] + term
             for k in range(4):
                 lanes = slice(k * 128, (k + 1) * 128)
                 negated = sums[k + 4]

time: 68.8 us -> 68.7 us (level)
  no operation moved by 1% of the time
where the time goes in v6:
time: 68.7 us; the launch traced here: 68.4 us
  waiting for transfers between devices  19.6 us (29%)
  blocking collectives  18.7 us (27%)
  Pallas kernels  18.2 us (26%)
  starting transfers between devices  7.72 us (11%)
  local copies, waits for them, and re-layouts  2.49 us (4%)
  other arithmetic  1.59 us (2%)
    all_to_all x1, waiting for transfers between devices, shards(): lax.all_to_all(rows.reshape(N, BPD * 256), 'scan', 0, 0, tiled=True)  19.6 us
    all_to_all x1, blocking collectives, shards(): lax.all_to_all(back.reshape(DET * SCAN, 2, 128), ('det', 'scan'), 0, 0, t...  18.7 us
    pallas_call x1, Pallas kernels, shards(): pl.pallas_call(phase_kernel, grid=(BPD,), in_specs=[smem, smem, smem], ou...  8.09 us
    all_to_all x1, starting transfers between devices, shards(): lax.all_to_all(rows.reshape(N, BPD * 256), 'scan', 0, 0, tiled=True)  7.72 us
    pallas_call x1, Pallas kernels, shards(): pl.pallas_call(column_kernel, in_specs=[smem, vmem, hbm, hbm, vmem], out_...  5.1 us
    pallas_call x1, Pallas kernels, shards(): pl.pallas_call(row_kernel, in_specs=[hbm, hbm], out_specs=hbm, out_shape=...  4.02 us
  transfers between devices with their start and end apart: 1, of which 1 were waited for; matrix products, arithmetic and copies ran while one was open for 6% of the time, Pallas kernels for 12%

profile of v6, /device:TPU:1, one launch (start us, length us, event | category | flops | bytes accessed | tf_op | source)
XLA Modules:
  0.0 68.4 jit_solution(9180513941849736644)
XLA Ops:
  0.0 0.0 copy-start
  0.0 4.0 %rows.1 = bf16[16,32,2304]{2,1,0:T(8,128)(2,1)} custom-call(bf16[72,32,512]{2,1,0:T(8,128)(2,1)} %x_hbm.1, bf16[512,512]{1,0:T(8,128)(2,1)} %constant.58.clone.table_hbm), custom_call_target="tpu_custom_call" | custom-call | tf_op jit(solution)/shard_map/rows/pallas_call | solution.py:361
  4.0 0.0 copy-start.4
  4.0 0.0 copy-start.3
  4.1 0.0 copy-start.1
  4.1 7.7 %all-to-all-start = ((bf16[16,32,2304]{2,1,0:T(8,128)(2,1)}), bf16[16,32,2304]{2,1,0:T(8,128)(2,1)S(1)}, u32[]{:S(2)}, u32[]{:S(2)}) async-start(bf16[16,32,2304]{2,1,0:T(8,128)(2,1)} %rows.1), calls=%async_computation | async-start | bytes 4718592 | tf_op jit(solution)/shard_map/all_to_all | solution.py:378
  11.8 0.1 compare_and_fusion
  11.9 0.0 copy-done
  11.9 1.2 %gather_fusion.1 = s32[3,8,16]{2,0,1:T(4,128)} fusion(s32[8,16,16]{2,1,0:T(8,128)S(1)} %copy-done, s32[1024]{0:T(1024)S(1)} %pad_clamp_fusion), kind=kCustom, calls=%fused_computation.1.clone | custom fusion | bytes 3084 | tf_op jit(solution)/shard_map/jit(_take)/gather | solution.py:344
  13.1 0.0 copy-done.4
  13.1 1.2 %gather_fusion = s32[3,8,16]{2,0,1:T(4,128)} fusion(s32[8,16,16]{2,1,0:T(8,128)S(1)} %copy-done.4, s32[1024]{0:T(1024)S(1)} %pad_clamp_fusion), kind=kCustom, calls=%fused_computation.clone | custom fusion | bytes 3084 | tf_op jit(solution)/shard_map/jit(_take)/gather | solution.py:343
  14.3 0.8 %select_bitcast_fusion.1 = (s32[8,3,16]{2,1,0:T(4,128)S(1)}, s32[8,3,16]{2,1,0:T(4,128)S(1)}) fusion(s32[3,8,16]{2,0,1:T(4,128)} %gather_fusion, pred[3]{0:T(512)(128)(4,1)S(1)} %get-tuple-element.10, s32[3,8,16]{2,0,1:T(4,128)} %gather_fusion.1), kind=kLoop, calls=%fused_computation.4 | loop fusion | flops 768 | bytes 6147 | tf_op jit(solution)/shard_map/jit(_take)/select_n | solution.py:343
  15.1 0.6 select_reduce_fusion
  15.7 0.1 reshape.24.flags_ref
  15.8 0.1 pad_add_fusion.meta_ref
  15.9 0.0 copy-done.3
  15.9 8.1 %phases.1 = (bf16[9,256,1024]{2,1,0:T(8,128)(2,1)}, bf16[512,256]{1,0:T(8,128)(2,1)}) custom-call(s32[2]{0:T(128)S(1)} %pad_add_fusion.meta_ref, s32[216]{0:T(256)S(1)} %reshape.24.flags_ref, f32[3]{0:T(128)S(1)} %copy-done.3), custom_call_target="tpu_custom_call" | custom-call | tf_op jit(solution)/shard_map/phases/pallas_call | solution.py:380
  24.0 19.6 %all-to-all-done = bf16[16,32,2304]{2,1,0:T(8,128)(2,1)S(1)} async-done(((bf16[16,32,2304]{2,1,0:T(8,128)(2,1)}), bf16[16,32,2304]{2,1,0:T(8,128)(2,1)S(1)}, u32[]{:S(2)}, u32[]{:S(2)}) %all-to-all-start) | async-done | bytes 2359328 | tf_op jit(solution)/shard_map/all_to_all | solution.py:378
  43.6 0.0 copy-done.1
  43.6 0.0 copy-start.2
  43.6 5.1 %columns.1 = bf16[256,128]{1,0:T(8,128)(2,1)S(1)} custom-call(s32[2]{0:T(128)S(1)} %pad_add_fusion.meta_ref, bf16[512,2304]{1,0:T(8,128)(2,1)S(1)} %bitcast.13, bf16[9,256,1024]{2,1,0:T(8,128)(2,1)} %get-tuple-element.8.phase_hbm, bf16[512,256]{1,0:T(8,128)(2,1)} %get-tuple-element.9.pick_hbm, bf16[1024,512]{1,0:T(8,128)(2,1)S(1)} %copy-done.1), custom_call_target="tpu_custom_call" | custom-call | tf_op jit(solution)/shard_map/columns/pallas_call | solution.py:390
  48.7 18.7 %all_to_all.13 = bf16[128,2,128]{2,1,0:T(2,128)(2,1)S(1)} all-to-all(bf16[128,2,128]{2,1,0:T(2,128)(2,1)S(1)} %bitcast.14), channel_id=1, replica_groups=mesh['det'=8,'scan'=16] {'det','scan'}, dimensions={0} | all-to-all | bytes 131072 | tf_op jit(solution)/shard_map/all_to_all | solution.py:408
  67.4 0.0 copy-done.2
  67.4 1.0 %last.1 = f32[2,4,512]{2,1,0:T(4,128)} custom-call(bf16[256,128]{1,0:T(8,128)(2,1)S(1)} %bitcast.15, bf16[512,1024]{1,0:T(8,128)(2,1)S(1)} %copy-done.2), custom_call_target="tpu_custom_call" | custom-call | tf_op jit(solution)/shard_map/last/pallas_call | solution.py:410
  (4 shorter events, 0.0 us)
Async XLA Ops:
  0.0 11.9 %copy-start = (s32[8,16,16]{2,1,0:T(8,128)S(1)}, s32[8,16,16]{2,1,0:T(8,128)}, u32[]{:S(2)}) copy-start(s32[8,16,16]{2,1,0:T(8,128)} %param.12) | copy-start | bytes 24580
  4.0 9.1 %copy-start.4 = (s32[8,16,16]{2,1,0:T(8,128)S(1)}, s32[8,16,16]{2,1,0:T(8,128)}, u32[]{:S(2)}) copy-start(s32[8,16,16]{2,1,0:T(8,128)} %param.11) | copy-start | bytes 24580
  4.0 11.9 %copy-start.3 = (f32[3]{0:T(128)S(1)}, f32[3]{0:T(128)}, u32[]{:S(2)}) copy-start(f32[3]{0:T(128)} %ab_ref.1) | copy-start | bytes 40
  4.1 39.6 %copy-start.1 = (bf16[1024,512]{1,0:T(8,128)(2,1)S(1)}, bf16[1024,512]{1,0:T(8,128)(2,1)}, u32[]{:S(2)}) copy-start(bf16[1024,512]{1,0:T(8,128)(2,1)} %constant.59.clone.table_ref) | copy-start | bytes 3145732
  4.1 39.6 %all-to-all-start = ((bf16[16,32,2304]{2,1,0:T(8,128)(2,1)}), bf16[16,32,2304]{2,1,0:T(8,128)(2,1)S(1)}, u32[]{:S(2)}, u32[]{:S(2)}) async-start(bf16[16,32,2304]{2,1,0:T(8,128)(2,1)} %rows.1), calls=%async_computation | async-start | bytes 4718592 | tf_op jit(solution)/shard_map/all_to_all | solution.py:378
  43.6 23.8 %copy-start.2 = (bf16[512,1024]{1,0:T(8,128)(2,1)S(1)}, bf16[512,1024]{1,0:T(8,128)(2,1)}, u32[]{:S(2)}) copy-start(bf16[512,1024]{1,0:T(8,128)(2,1)} %constant.60.clone.table_ref) | copy-start | bytes 3145732
